TPU v7x, 128 devices: a whole 4x4x4 slice. The times are simulated.
128 devices in a mesh: blk: 16 (over z, x_lo, core), expert: 8 (over x_hi, y).
Axes of the slice: x: 4 (x_hi: 2, x_lo: 2; x = x_hi * 2 + x_lo), y: 4, z: 4, core: 2. Of those that a mesh axis runs over, the one named last changes fastest.
Arguments:
- new_tokens: bfloat16 [8, 2048, 2048], P('expert', 'blk'), may hold values from -6 to 6
- norm_gain: float32 [2048], replicated, may hold values from 0.5 to 1.5
- router_weight: bfloat16 [2048, 8], replicated, may hold values from -0.125 to 0.125
- att_choice: int32 [8, 2048, 2], P('expert', 'blk'), may hold values from 0 to 7, all different within a row; in each aligned block of 128 rows (0 to 127, 128 to 255, ..., all dimensions but the last counted through in order) at most 64 rows name the same one
- w_query: bfloat16 [8, 2048, 1024], P('expert'), may hold values from -0.125 to 0.125
- w_key: bfloat16 [2048, 1024], replicated, may hold values from -0.375 to 0.375
- w_value: bfloat16 [2048, 1024], replicated, may hold values from -0.125 to 0.125
- w_out: bfloat16 [8, 1024, 2048], P('expert'), may hold values from -0.1875 to 0.1875
- cache_keys: bfloat16 [8, 5120, 1024], P('expert', 'blk'), may hold values from -12 to 12
- cache_values: bfloat16 [8, 5120, 1024], P('expert', 'blk'), may hold values from -6 to 6
- hidden_held: bfloat16 [8, 512, 2048], P('expert', 'blk'), may hold values from -6 to 6
- recompute_ids: int32 [8, 16], P('expert', 'blk'), may hold values from 0 to 9
- block_live: int32 [8, 160], P('expert', 'blk'), may hold values 0 or 1
- cached_len: int32 [8], P('expert'), may hold values from 1 to 5120, as said below
Outputs:
- layer_out: bfloat16 [8, 2048, 2048], P('expert', 'blk')
Inputs may be any that keep to these rules, and one draw needn't show every extreme that they name: `att_choice`: a token's two choices differ; among the tokens of one index of blk and expert, at most 64 name any one expert. `cached_len`: one request in every draw has exactly 5120 cached tokens.
All inputs are finite; a program needn't handle non-finite values. No bound on the sum of `block_live` on one device may be relied on, other than what follows from the above.
Results may differ from a plain program's by a relative error of at most 0.012.
Values may be sent and summed in bfloat16 or wider, within the bound.
A program may use at most 192 MiB of HBM per device.

v0:
```python
import math

import jax
import jax.numpy as jnp
from jax import lax
from jax.sharding import PartitionSpec as P

HD = 128
KVH = 8
CB = 32
CAP = 64


epsilon = 1e-06
theta_base = 10000.0
far_position = 1073741824


def normalize(hidden, norm_gain):
    widened = hidden.astype(jnp.float32)
    inverse = lax.rsqrt(jnp.mean(widened * widened, axis=-1, keepdims=True) + epsilon)
    return (widened * inverse * norm_gain).astype(jnp.bfloat16)


def rotate(projected, positions):
    row_count = projected.shape[0]
    half_width = HD // 2
    separated = projected.reshape(row_count, KVH, HD)
    frequency = jnp.exp(
        jnp.arange(half_width, dtype=jnp.float32) * (-math.log(theta_base) / half_width)
    )
    angles = positions.astype(jnp.float32)[:, None] * frequency[None, :]
    cosine = jnp.cos(angles)[:, None, :]
    sine_part = jnp.sin(angles)[:, None, :]
    first_half = separated[..., :half_width]
    second_half = separated[..., half_width:]
    turned = jnp.concatenate(
        [
            first_half * cosine - second_half * sine_part,
            second_half * cosine + first_half * sine_part,
        ],
        axis=-1,
    )
    return turned.reshape(row_count, KVH * HD)


def attend(queries, query_pos, key_rows, value_rows, key_pos):
    score_scale = 1.0 / math.sqrt(HD)
    key_heads = key_rows.reshape(key_rows.shape[0], KVH, HD)
    value_heads = value_rows.reshape(value_rows.shape[0], KVH, HD)
    scores = (
        jnp.einsum("qhd,khd->qhk", queries, key_heads, preferred_element_type=jnp.float32)
        * score_scale
    )
    allowed = key_pos[None, None, :] <= query_pos[:, None, None]
    weights = jnp.where(allowed, jnp.exp(scores), 0.0).astype(jnp.bfloat16)
    denominator = jnp.sum(weights, axis=-1, dtype=jnp.float32)
    numerator = jnp.einsum("qhk,khd->qhd", weights, value_heads, preferred_element_type=jnp.float32)
    return (numerator, denominator)


def shards(
    new_tokens,
    norm_gain,
    router_weight,
    att_choice,
    w_query,
    w_key,
    w_value,
    w_out,
    cache_keys,
    cache_values,
    hidden_held,
    recompute_ids,
    block_live,
    cached_len,
):
    blk_index = lax.axis_index("blk")
    length = cached_len[0]
    tokens = new_tokens[0]
    row_count = tokens.shape[0]
    cache_len = cache_keys.shape[1]
    experts = lax.axis_size("expert") * w_query.shape[0]
    capacity = CAP
    key_width = KVH * HD
    normed = normalize(tokens, norm_gain)
    held_norm = normalize(hidden_held[0], norm_gain)
    new_pos = length + blk_index * row_count + jnp.arange(row_count, dtype=jnp.int32)
    held_start = recompute_ids[0, 0] * CB
    held_pos = blk_index * cache_len + held_start + jnp.arange(CB, dtype=jnp.int32)
    both_rows = jnp.concatenate([normed, held_norm], axis=0)
    both_pos = jnp.concatenate([new_pos, held_pos])
    key_proj = rotate(
        jnp.dot(both_rows, w_key, preferred_element_type=jnp.float32), both_pos
    ).astype(jnp.bfloat16)
    value_proj = jnp.dot(both_rows, w_value, preferred_element_type=jnp.float32).astype(
        jnp.bfloat16
    )
    cached_keys = lax.dynamic_update_slice_in_dim(
        cache_keys[0], key_proj[row_count:], held_start, 0
    )
    cached_values = lax.dynamic_update_slice_in_dim(
        cache_values[0], value_proj[row_count:], held_start, 0
    )
    local_keys = jnp.concatenate([cached_keys, key_proj[:row_count]], axis=0)
    local_values = jnp.concatenate([cached_values, value_proj[:row_count]], axis=0)
    slot_pos = blk_index * cache_len + jnp.arange(cache_len, dtype=jnp.int32)
    live_flags = jnp.repeat(block_live[0], CB)
    usable = (slot_pos < length) & (live_flags == 1)
    local_pos = jnp.concatenate([jnp.where(usable, slot_pos, far_position), new_pos])
    picked = att_choice[0].reshape(-1)
    one_hot = (picked[:, None] == jnp.arange(experts, dtype=jnp.int32)[None, :]).astype(jnp.int32)
    before = jnp.cumsum(one_hot, axis=0) - one_hot
    slot_index = jnp.sum(before * one_hot, axis=1)
    target = picked * capacity + slot_index
    logits = jnp.dot(normed, router_weight, preferred_element_type=jnp.float32)
    chosen = jnp.sum(
        jnp.where(one_hot.reshape(row_count, 2, experts) == 1, logits[:, None, :], 0.0), axis=2
    )
    gate_first = jax.nn.sigmoid(chosen[:, 0] - chosen[:, 1])
    send_rows = (
        jnp.zeros((experts * capacity, tokens.shape[1]), jnp.bfloat16)
        .at[target]
        .set(jnp.repeat(normed, 2, axis=0))
    )
    send_pos = jnp.zeros((experts * capacity,), jnp.int32).at[target].set(jnp.repeat(new_pos, 2))
    incoming = lax.all_to_all(
        send_rows.reshape(experts, capacity, -1), "expert", split_axis=0, concat_axis=0, tiled=True
    )
    incoming_pos = lax.all_to_all(
        send_pos.reshape(experts, capacity), "expert", split_axis=0, concat_axis=0, tiled=True
    )
    sources, slot_count, row_width = incoming.shape
    projected = jnp.dot(
        incoming.reshape(sources * slot_count, row_width),
        w_query[0],
        preferred_element_type=jnp.float32,
    )
    turned = (
        rotate(projected, incoming_pos.reshape(-1))
        .astype(jnp.bfloat16)
        .reshape(sources, slot_count, key_width)
    )
    queries_back = lax.all_to_all(turned, "expert", split_axis=0, concat_axis=0, tiled=True)
    query_rows = queries_back.reshape(experts * capacity, key_width)[target]
    all_rows = 2 * row_count
    query_heads = query_rows.reshape(all_rows, KVH, HD)
    query_pos = jnp.repeat(new_pos, 2)
    piece_keys = lax.all_gather(local_keys, "blk", axis=0, tiled=True)
    piece_values = lax.all_gather(local_values, "blk", axis=0, tiled=True)
    piece_pos = lax.all_gather(local_pos, "blk", axis=0, tiled=True)
    part_num, part_den = attend(query_heads, query_pos, piece_keys, piece_values, piece_pos)
    attended = (part_num / part_den[..., None]).astype(jnp.bfloat16).reshape(all_rows, key_width)
    send_out = jnp.zeros((experts * capacity, key_width), jnp.bfloat16).at[target].set(attended)
    received = lax.all_to_all(
        send_out.reshape(experts, capacity, key_width),
        "expert",
        split_axis=0,
        concat_axis=0,
        tiled=True,
    )
    sources, slot_count, row_width = received.shape
    projected = jnp.dot(
        received.reshape(sources * slot_count, row_width),
        w_out[0],
        preferred_element_type=jnp.float32,
    )
    returned = lax.all_to_all(
        projected.astype(jnp.bfloat16).reshape(sources, slot_count, -1),
        "expert",
        split_axis=0,
        concat_axis=0,
        tiled=True,
    )
    expert_out = (
        returned.reshape(experts * capacity, -1)[target]
        .reshape(row_count, 2, -1)
        .astype(jnp.float32)
    )
    combined = (
        tokens.astype(jnp.float32)
        + gate_first[:, None] * expert_out[:, 0]
        + (1.0 - gate_first)[:, None] * expert_out[:, 1]
    )
    return combined.astype(jnp.bfloat16)[None]


def solution(mesh):
    placed = (
        P("expert", "blk", None),
        P(),
        P(),
        P("expert", "blk", None),
        P("expert", None, None),
        P(),
        P(),
        P("expert", None, None),
        P("expert", "blk", None),
        P("expert", "blk", None),
        P("expert", "blk", None),
        P("expert", "blk"),
        P("expert", "blk"),
        P("expert"),
    )
    return jax.shard_map(
        shards, mesh=mesh, in_specs=placed, out_specs=P("expert", "blk", None), check_vma=False
    )
```

profile of v0, /device:TPU:0, one launch (start us, length us, event | category | flops | bytes accessed | tf_op | source)
XLA Modules:
  0.0 328.8 jit_solution(7634905290585062930)
XLA Ops:
  8.0 1.2 fusion.10
  9.2 1.0 fusion.23
  10.2 1.2 fusion.12
  11.6 3.0 convolution_bitcast_fusion.1
  14.8 0.4 multiply_cosine_fusion.1
  15.2 0.3 subtract_convert_fusion.1
  15.6 0.1 pad_maximum_fusion.6
  15.9 1.0 pad_maximum_fusion.2
  16.9 3.0 convolution_convert_fusion
  20.0 1.0 pad_maximum_fusion.1
  21.5 0.6 reduce-window.6
  22.1 0.2 slice_reduce_fusion
  22.9 1.4 scatter_custom_fusion.1
  24.3 0.7 all_to_all.19
  25.0 7.0 %all-to-all-start.1 = ((s32[8,1,64]{2,1,0:T(1,128)}), s32[8,1,64]{2,1,0:T(1,128)S(1)}, u32[]{:S(2)}, u32[]{:S(2)}) async-start(s32[8,1,64]{2,1,0:T(1,128)} %all_to_all.19), calls=%async_computation.1 | async-start | bytes 8192 | tf_op jit(solution)/shard_map/all_to_all | solution.py:130
  32.0 0.6 broadcast_in_dim.48
  32.7 0.4 reshape.405
  33.1 3.7 %scatter_custom_fusion = bf16[512,2048]{1,0:T(8,128)(2,1)} fusion(s32[256]{0:T(256)S(1)} %bitcast.130, bf16[256,2048]{1,0:T(8,128)(2,1)S(1)} %reshape.405, bf16[]{:T(256)} %constant.22.clone.1), kind=kCustom, calls=%fused_computation.33 | custom fusion | bytes 2097154 | tf_op jit(solution)/shard_map/scatter | solution.py:124
  36.8 2.8 all-to-all-done.1
  39.6 4.4 %all-to-all-start = ((bf16[8,64,2048]{2,1,0:T(8,128)(2,1)}), bf16[8,64,2048]{2,1,0:T(8,128)(2,1)S(1)}, u32[]{:S(2)}, u32[]{:S(2)}) async-start(bf16[8,64,2048]{2,1,0:T(8,128)(2,1)} %bitcast.17), calls=%async_computation | async-start | bytes 4194304 | tf_op jit(solution)/shard_map/all_to_all | solution.py:127
  44.0 6.5 %copy.71 = bf16[1024,2048]{1,0:T(8,128)(2,1)} copy(bf16[1024,2048]{0,1:T(8,128)(2,1)} %bitcast.116) | data formatting | bytes 8388608 | tf_op jit(solution)/shard_map/dot_general | solution.py:134
  50.7 0.6 dynamic-slice
  52.0 0.2 add_dynamic-update-slice_fusion
  52.2 88.5 %all-reduce = s32[7168]{0:T(1024)S(1)} all-reduce(s32[7168]{0:T(1024)S(1)} %add_dynamic-update-slice_fusion), channel_id=1, replica_groups=mesh['blk'=16,'expert'=8] {'blk'}, use_global_device_ids=true, to_apply=%add | all-reduce | flops 7168 | bytes 57344
  140.8 0.5 multiply_cosine_fusion
  141.3 4.7 %fusion.38 = f32[512,8,128]{0,2,1:T(8,128)S(1)} fusion(bf16[512,2048,1]{1,0,2:T(8,128)(2,1)S(1)} %bitcast.121, bf16[8,128,2048]{2,1,0:T(8,128)(2,1)} %bitcast.117), kind=kOutput, calls=%fused_computation.92 | convolution fusion | flops 2147483648 | bytes 8388608 | tf_op jit(solution)/shard_map/dot_general | solution.py:134
  146.0 0.4 subtract_convert_fusion
  146.5 0.8 copy.62
  147.3 1.3 convert_element_type.95
  148.5 7.3 %all-to-all-start.2 = ((bf16[8,64,1024]{2,1,0:T(8,128)(2,1)}), bf16[8,64,1024]{2,1,0:T(8,128)(2,1)S(1)}, u32[]{:S(2)}, u32[]{:S(2)}) async-start(bf16[8,64,1024]{2,1,0:T(8,128)(2,1)} %convert_element_type.95), calls=%async_computation.2 | async-start | bytes 2097152 | tf_op jit(solution)/shard_map/all_to_all | solution.py:144
  155.8 4.2 %broadcast_compare_fusion = pred[256,7168]{0,1:T(8,128)(4,1)} fusion(s32[256]{0:T(256)S(1)} %reshape.413, s32[7168]{0:T(1024)S(1)} %all-reduce), kind=kLoop, calls=%fused_computation.10 | loop fusion | flops 1835008 | bytes 1864704 | tf_op jit(solution)/shard_map/le | solution.py:55
  160.0 21.8 %all-to-all-done.2 = bf16[8,64,1024]{2,1,0:T(8,128)(2,1)S(1)} async-done(((bf16[8,64,1024]{2,1,0:T(8,128)(2,1)}), bf16[8,64,1024]{2,1,0:T(8,128)(2,1)S(1)}, u32[]{:S(2)}, u32[]{:S(2)}) %all-to-all-start.2) | async-done | bytes 1048608 | tf_op jit(solution)/shard_map/all_to_all | solution.py:144
  181.8 1.2 gather_fusion
  183.0 18.9 %copy.60 = bf16[7168,1024]{0,1:T(8,128)(2,1)} copy(bf16[7168,1024]{1,0:T(8,128)(2,1)} %all-gather.5.cloned.1.call-done) | data formatting | bytes 29360128 | tf_op jit(solution)/shard_map/all_gather | solution.py:149
  202.0 21.5 %convert_reduce_fusion = (f32[256,8]{0,1:T(8,128)S(1)}, bf16[256,8,7168]{0,2,1:T(8,128)(2,1)}) fusion(bf16[7168,8,128]{0,2,1:T(8,128)(2,1)} %bitcast.113, pred[256,7168]{0,1:T(8,128)(4,1)S(1)} %copy-done.4, bf16[256,1024]{1,0:T(8,128)(2,1)S(1)} %gather_fusion), kind=kOutput, calls=%fused_computation.7 | convolution fusion | flops 3831494656 | bytes 46407680 | tf_op jit(solution)/shard_map/qhd,khd->qhk/dot_general | solution.py:52
  223.4 18.4 %copy.59 = bf16[7168,1024]{0,1:T(8,128)(2,1)} copy(bf16[7168,1024]{1,0:T(8,128)(2,1)} %all-gather.3.cloned.1.call-done) | data formatting | bytes 29360128 | tf_op jit(solution)/shard_map/all_gather | solution.py:150
  241.8 15.7 %fusion.9 = bf16[256,8,128]{0,2,1:T(8,128)(2,1)S(1)} fusion(bf16[7168,8,128]{0,2,1:T(8,128)(2,1)} %bitcast.114, bf16[256,8,7168]{0,2,1:T(8,128)(2,1)} %get-tuple-element.18, f32[256,8]{0,1:T(8,128)S(1)} %get-tuple-element.17), kind=kOutput, calls=%fused_computation.18 | convolution fusion | flops 3758620672 | bytes 44572672 | tf_op jit(solution)/shard_map/qhk,khd->qhd/dot_general | solution.py:58
  257.5 0.2 copy.66
  257.7 1.9 scatter_custom_fusion.2
  259.7 20.3 %all_to_all.29 = bf16[8,64,1024]{2,1,0:T(8,128)(2,1)S(1)} all-to-all(bf16[8,64,1024]{2,1,0:T(8,128)(2,1)S(1)} %bitcast.118), channel_id=1, replica_groups=mesh['blk'=16,'expert'=8] {'expert'}, dimensions={0} | all-to-all | bytes 2097152 | tf_op jit(solution)/shard_map/all_to_all | solution.py:155
  280.0 5.9 %fusion.3 = bf16[512,2048]{1,0:T(8,128)(2,1)} fusion(bf16[512,1024]{1,0:T(8,128)(2,1)S(1)} %bitcast.125, bf16[1,1024,2048]{2,1,0:T(8,128)(2,1)} %param.21), kind=kOutput, calls=%fused_computation.11 | convolution fusion | flops 2148532224 | bytes 7340032 | tf_op jit(solution)/shard_map/dot_general | solution.py:163
  285.8 3.8 %all-to-all-start.4 = ((bf16[8,64,2048]{2,1,0:T(8,128)(2,1)}), bf16[8,64,2048]{2,1,0:T(8,128)(2,1)S(1)}, u32[]{:S(2)}, u32[]{:S(2)}) async-start(bf16[8,64,2048]{2,1,0:T(8,128)(2,1)} %bitcast.122), calls=%async_computation.4 | async-start | bytes 4194304 | tf_op jit(solution)/shard_map/all_to_all | solution.py:168
  289.7 0.2 fusion.37
  290.0 23.6 %all-to-all-done.4 = bf16[8,64,2048]{2,1,0:T(8,128)(2,1)S(1)} async-done(((bf16[8,64,2048]{2,1,0:T(8,128)(2,1)}), bf16[8,64,2048]{2,1,0:T(8,128)(2,1)S(1)}, u32[]{:S(2)}, u32[]{:S(2)}) %all-to-all-start.4) | async-done | bytes 2097184 | tf_op jit(solution)/shard_map/all_to_all | solution.py:168
  313.6 2.3 gather_fusion.1
  315.9 2.4 reshape.384
  318.4 1.6 fusion.36
  320.0 1.9 fusion.14
  (64 shorter events, 2.0 us)
Async XLA Ops:
  6.5 283.1 %copy-start = (bf16[2048,8]{0,1:T(8,128)(2,1)S(1)}, bf16[2048,8]{0,1:T(8,128)(2,1)}, u32[]{:S(2)}) copy-start(bf16[2048,8]{0,1:T(8,128)(2,1)} %param.16) | copy-start | bytes 98308
  6.5 5.0 %copy-start.6 = (f32[2048]{0:T(1024)S(1)}, f32[2048]{0:T(1024)}, u32[]{:S(2)}) copy-start(f32[2048]{0:T(1024)} %param.15) | copy-start | bytes 24580
  6.5 5.0 %copy-start.5 = (bf16[1,32,2048]{2,1,0:T(8,128)(2,1)S(1)}, bf16[1,32,2048]{2,1,0:T(8,128)(2,1)}, u32[]{:S(2)}) copy-start(bf16[1,32,2048]{2,1,0:T(8,128)(2,1)} %param.24) | copy-start | bytes 393220
  6.5 176.5 %all-gather.5.cloned.1.call-start = ((), (), s32[]{:S(2)}) async-start(), calls=%async_computation.6 | async-start | bytes 15597568 | tf_op jit(solution)/shard_map/all_gather | solution.py:149
  14.7 1.2 copy-start.3
  15.8 4.2 %copy-start.2 = (bf16[1,320,1024]{2,1,0:T(8,128)(2,1)S(1)}, bf16[1,320,1024]{2,1,0:T(8,128)(2,1)}, u32[]{:S(2)}) copy-start(bf16[1,320,1024]{2,1,0:T(8,128)(2,1)} %param.23) | copy-start | bytes 1966084
  16.9 4.2 %copy-start.7 = (s32[1,128,2]{1,2,0:T(2,128)S(1)}, s32[1,128,2]{1,2,0:T(2,128)}, u32[]{:S(2)}) copy-start(s32[1,128,2]{1,2,0:T(2,128)} %param.17) | copy-start | bytes 3076
  16.9 206.5 %all-gather.3.cloned.1.call-start = ((), (), s32[]{:S(2)}) async-start(), calls=%async_computation.5 | async-start | bytes 15597568 | tf_op jit(solution)/shard_map/all_gather | solution.py:150
  25.0 14.6 %all-to-all-start.1 = ((s32[8,1,64]{2,1,0:T(1,128)}), s32[8,1,64]{2,1,0:T(1,128)S(1)}, u32[]{:S(2)}, u32[]{:S(2)}) async-start(s32[8,1,64]{2,1,0:T(1,128)} %all_to_all.19), calls=%async_computation.1 | async-start | bytes 8192 | tf_op jit(solution)/shard_map/all_to_all | solution.py:130
  39.6 101.7 %all-to-all-start = ((bf16[8,64,2048]{2,1,0:T(8,128)(2,1)}), bf16[8,64,2048]{2,1,0:T(8,128)(2,1)S(1)}, u32[]{:S(2)}, u32[]{:S(2)}) async-start(bf16[8,64,2048]{2,1,0:T(8,128)(2,1)} %bitcast.17), calls=%async_computation | async-start | bytes 4194304 | tf_op jit(solution)/shard_map/all_to_all | solution.py:127
  44.0 6.6 %copy-start.8 = (s32[1,10]{1,0:T(1,128)S(1)}, s32[1,10]{1,0:T(1,128)}, u32[]{:S(2)}) copy-start(s32[1,10]{1,0:T(1,128)} %param.26) | copy-start | bytes 124
  44.0 6.7 %copy-start.9 = (u32[128]{0:T(128)S(1)}, u32[128]{0:T(128)}, u32[]{:S(2)}) copy-start(u32[128]{0:T(128)} %constant.61) | copy-start | bytes 1540
  148.5 33.3 %all-to-all-start.2 = ((bf16[8,64,1024]{2,1,0:T(8,128)(2,1)}), bf16[8,64,1024]{2,1,0:T(8,128)(2,1)S(1)}, u32[]{:S(2)}, u32[]{:S(2)}) async-start(bf16[8,64,1024]{2,1,0:T(8,128)(2,1)} %convert_element_type.95), calls=%async_computation.2 | async-start | bytes 2097152 | tf_op jit(solution)/shard_map/all_to_all | solution.py:144
  183.0 19.0 %copy-start.4 = (pred[256,7168]{0,1:T(8,128)(4,1)S(1)}, pred[256,7168]{0,1:T(8,128)(4,1)}, u32[]{:S(2)}) copy-start(pred[256,7168]{0,1:T(8,128)(4,1)} %broadcast_compare_fusion) | copy-start | bytes 5505028
  285.8 27.7 %all-to-all-start.4 = ((bf16[8,64,2048]{2,1,0:T(8,128)(2,1)}), bf16[8,64,2048]{2,1,0:T(8,128)(2,1)S(1)}, u32[]{:S(2)}, u32[]{:S(2)}) async-start(bf16[8,64,2048]{2,1,0:T(8,128)(2,1)} %bitcast.122), calls=%async_computation.4 | async-start | bytes 4194304 | tf_op jit(solution)/shard_map/all_to_all | solution.py:168
  315.9 4.1 %copy-start.1 = (bf16[1,128,2048]{2,1,0:T(8,128)(2,1)S(1)}, bf16[1,128,2048]{2,1,0:T(8,128)(2,1)}, u32[]{:S(2)}) copy-start(bf16[1,128,2048]{2,1,0:T(8,128)(2,1)} %param.14) | copy-start | bytes 1572868
Sparse Core Ops, SparseCore 0:
  17.0 107.4 all-gather.4
  126.2 93.6 all-gather.2
where the time goes:
time: 331 us; the launch traced here: 329 us
  blocking collectives  109 us (33%)
  local copies, waits for them, and re-layouts  64.6 us (20%)
  matrix products  54 us (16%)
  waiting for transfers between devices  48.3 us (15%)
  starting transfers between devices  22.6 us (7%)
  between operations  15.8 us (5%)
  other arithmetic  14.7 us (4%)
    unnamed x1, blocking collectives  88.5 us
    all_to_all x1, waiting for transfers between devices, shards(): lax.all_to_all(projected.astype(jnp.bfloat16).reshape(sources, slot_count...  23.6 us
    all_to_all x1, waiting for transfers between devices, shards(): lax.all_to_all(turned, 'expert', split_axis=0, concat_axis=0, tiled=True)  21.8 us
    dot_general x1, matrix products, attend(): jnp.einsum('qhd,khd->qhk', queries, key_heads, preferred_element_type=jnp...  21.5 us
    all_to_all x1, blocking collectives, shards(): lax.all_to_all(send_out.reshape(experts, capacity, key_width), 'expert',...  20.3 us
    all_gather x1, local copies, waits for them, and re-layouts, shards(): piece_keys = lax.all_gather(local_keys, 'blk', axis=0, tiled=True)  18.9 us
    all_gather x1, local copies, waits for them, and re-layouts, shards(): piece_values = lax.all_gather(local_values, 'blk', axis=0, tiled=True)  18.4 us
    dot_general x1, matrix products, attend(): jnp.einsum('qhk,khd->qhd', weights, value_heads, preferred_element_type=j...  15.7 us
  transfers between devices with their start and end apart: 6, of which 3 were waited for; matrix products, arithmetic and copies ran while one was open for 22% of the time, Pallas kernels for 0%

commit v1 on v0

v1 whole, which is shorter than its diff:
```python
import functools
import math

import jax
import jax.numpy as jnp
from jax import lax
from jax.experimental import pallas as pl
from jax.experimental.pallas import tpu as pltpu
from jax.sharding import PartitionSpec as P

HD = 128
KVH = 8
CB = 32
CAP = 64
D = 2048
KVW = KVH * HD
NEW_DEV = 128
CACHE_DEV = 320
KEYS = NEW_DEV + CACHE_DEV
HALF = KEYS // 2
EXPERTS = 8
SLOTS = EXPERTS * CAP
ROWS = 2 * NEW_DEV
KC = 4
KW = D // KC
NC = 4
NW = D // NC
NZ = 4

epsilon = 1e-06
theta_base = 10000.0
MASKED = -1e30
LOG2E = 1.4426950408889634
SCALE = LOG2E / math.sqrt(HD)


def normalize(hidden, norm_gain):
    widened = hidden.astype(jnp.float32)
    inverse = lax.rsqrt(jnp.mean(widened * widened, axis=-1, keepdims=True) + epsilon)
    return (widened * inverse * norm_gain).astype(jnp.bfloat16)


def rope_tables(positions):
    half_width = HD // 2
    frequency = jnp.exp(
        jnp.arange(half_width, dtype=jnp.float32) * (-math.log(theta_base) / half_width)
    )
    angles = positions.astype(jnp.float32)[:, None] * frequency[None, :]
    cosine = jnp.cos(angles)
    sine = jnp.sin(angles)
    return jnp.concatenate([cosine, cosine], 1), jnp.concatenate([-sine, sine], 1)


def rotate(projected, cosine, sine):
    row_count = projected.shape[0]
    half_width = HD // 2
    v = projected.reshape(row_count, KVH, HD)
    swapped = jnp.concatenate([v[..., half_width:], v[..., :half_width]], axis=-1)
    return v * cosine[:, None, :] + swapped * sine[:, None, :]


def kernel(
    kv_own,
    bias_own,
    rows_send,
    gather_q,
    spread_q,
    gates,
    cosine,
    sine,
    tokens,
    w_query,
    w_out,
    out,
    kv,
    bias,
    rows,
    wq,
    wo,
    qacc,
    qsend,
    qret,
    queries,
    acc,
    own_part,
    num_send,
    num_recv,
    den_send,
    den_recv,
    att_send,
    att_recv,
    exp_send,
    exp_recv,
    local_sem,
    rows_s,
    rows_r,
    qs_s,
    qs_r,
    kv_s,
    kv_r,
    bias_s,
    bias_r,
    qx_s,
    qx_r,
    num_s,
    num_r,
    den_s,
    den_r,
    att_s,
    att_r,
    exp_s,
    exp_r,
):
    blk = lax.axis_index("blk")
    expert = lax.axis_index("expert")
    z = blk // 4
    xl = (blk // 2) % 2
    c = blk % 2
    xh = expert // 4
    y = expert % 4

    def at_blk(zz, xx, cc):
        return {"blk": zz * 4 + xx * 2 + cc, "expert": expert}

    def peer(off):
        return ((xh + off // 4) % 2) * 4 + (y + off % 4) % 4

    def at_expert(e):
        return {"blk": blk, "expert": e}

    zp = (z + 1) % NZ
    zm = (z + NZ - 1) % NZ
    zo = (z + 2) % NZ
    up = at_blk(zp, xl, c)
    down = at_blk(zm, xl, c)
    partner = at_blk(z, xl, 1 - c)
    across = at_blk(z, 1 - xl, c)
    mine = z * 2 + c

    def remote(src, dst, ssem, rsem, device):
        return pltpu.make_async_remote_copy(
            src_ref=src,
            dst_ref=dst,
            send_sem=ssem,
            recv_sem=rsem,
            device_id=device,
            device_id_type=pl.DeviceIdType.MESH,
        )

    barrier = pltpu.get_barrier_semaphore()
    for off in range(1, 8):
        pl.semaphore_signal(
            barrier, inc=1, device_id=at_expert(peer(off)), device_id_type=pl.DeviceIdType.MESH
        )
        pl.semaphore_signal(
            barrier,
            inc=1,
            device_id=at_blk((z + off // 2) % NZ, xl, (c + off % 2) % 2),
            device_id_type=pl.DeviceIdType.MESH,
        )
    pl.semaphore_signal(barrier, inc=1, device_id=across, device_id_type=pl.DeviceIdType.MESH)

    load_wq = pltpu.make_async_copy(w_query, wq, local_sem.at[0])
    load_wo = pltpu.make_async_copy(w_out, wo, local_sem.at[1])
    load_kv = pltpu.make_async_copy(kv_own, kv.at[:, mine], local_sem.at[2])
    load_wq.start()
    load_kv.start()
    load_wo.start()
    pl.semaphore_wait(barrier, 15)

    def rows_copy(k, off):
        e = peer(off)
        return remote(
            rows_send.at[e, :, pl.ds(pl.multiple_of(k * KW, KW), KW)],
            rows.at[k, expert],
            rows_s.at[k, off],
            rows_r.at[k, off],
            at_expert(e),
        )

    def rows_local(k):
        return pltpu.make_async_copy(
            rows_send.at[expert, :, pl.ds(pl.multiple_of(k * KW, KW), KW)],
            rows.at[k, expert],
            local_sem.at[3 + k],
        )

    def kv_own_copy(h, way):
        return remote(
            kv_own.at[h],
            kv.at[h, mine],
            kv_s.at[h, way],
            kv_r.at[h, way],
            (up, down, partner)[way],
        )

    def kv_forward(h, way):
        source = (zm, zp)[way] * 2 + c
        part = pl.ds(way * HALF, HALF)
        return remote(
            kv.at[h, source, part],
            kv.at[h, source, part],
            kv_s.at[h, 3 + way],
            kv_r.at[h, 3 + way],
            (up, down)[way],
        )

    def kv_share(h, which):
        if which < 2:
            ref = kv.at[h, (zm, zp)[which] * 2 + c]
        else:
            ref = kv.at[h, zo * 2 + c, pl.ds((which - 2) * HALF, HALF)]
        return remote(ref, ref, kv_s.at[h, 5 + which], kv_r.at[h, 5 + which], partner)

    def bias_copy(off):
        return remote(
            bias_own,
            bias.at[mine],
            bias_s.at[off],
            bias_r.at[off],
            at_blk((z + off // 2) % NZ, xl, (c + off % 2) % 2),
        )

    def send_rows(k, _):
        for off in range(1, 8):
            rows_copy(k, off).start()
        rows_local(k).start()
        return 0

    lax.fori_loop(0, KC, send_rows, 0)

    def send_kv(h, _):
        for way in range(3):
            kv_own_copy(h, way).start()
        return 0

    lax.fori_loop(0, KVH, send_kv, 0)
    for off in range(1, 8):
        bias_copy(off).start()
    bias[mine] = bias_own[...]

    load_wq.wait()

    def project(k, _):
        for off in range(1, 8):
            rows_copy(k, off).wait_recv()
        rows_local(k).wait()
        part = jnp.dot(
            rows[k].reshape(SLOTS, KW),
            wq[pl.ds(pl.multiple_of(k * KW, KW), KW), :],
            preferred_element_type=jnp.float32,
        )

        @pl.when(k == 0)
        def _():
            qacc[...] = part

        @pl.when(k > 0)
        def _():
            qacc[...] += part

        return 0

    lax.fori_loop(0, KC, project, 0)
    qsend[...] = qacc[...].astype(jnp.bfloat16).reshape(EXPERTS, CAP, KVW)

    def q_copy(off):
        r = peer(off)
        return remote(
            qsend.at[r], qret.at[expert], qs_s.at[off], qs_r.at[off], at_expert(r)
        )

    for off in range(1, 8):
        q_copy(off).start()
    q_local = pltpu.make_async_copy(qsend.at[expert], qret.at[expert], local_sem.at[7])
    q_local.start()

    def pass_on(h, _):
        for way in range(2):
            kv_own_copy(h, way).wait_recv()
            kv_forward(h, way).start()
        for way in range(2):
            kv_share(h, way).start()
        return 0

    lax.fori_loop(0, KVH, pass_on, 0)

    for off in range(1, 8):
        q_copy(off).wait_recv()
    q_local.wait()
    gathered = jnp.dot(
        gather_q[...], qret[...].reshape(SLOTS, KVW), preferred_element_type=jnp.float32
    )
    for h in range(KVH):
        v = gathered[:, h * HD : (h + 1) * HD]
        turned = v * cosine[...] + pltpu.roll(v, HD // 2, 1) * sine[...]
        queries[h, 0:ROWS] = turned.astype(jnp.bfloat16)

    def qx_copy(h):
        return remote(
            queries.at[h, pl.ds(0, ROWS)],
            queries.at[h, pl.ds(ROWS, ROWS)],
            qx_s.at[h],
            qx_r.at[h],
            across,
        )

    for h in range(KVH):
        qx_copy(h).start()
    for off in range(1, 8):
        bias_copy(off).wait_recv()
    load_kv.wait()

    lead = (
        lax.broadcasted_iota(jnp.int32, (ROWS, NEW_DEV), 0) % NEW_DEV
        - lax.broadcasted_iota(jnp.int32, (ROWS, NEW_DEV), 1)
    )

    def block(h, zz, cc):
        j = zz * 2 + cc
        keys = kv[h, j, :, 0:HD]
        values = kv[h, j, :, HD : 2 * HD]
        scores = lax.dot_general(
            queries[h], keys, (((1,), (1,)), ((), ())), preferred_element_type=jnp.float32
        )
        offset_own = jnp.clip((j - mine) * NEW_DEV, -NEW_DEV, NEW_DEV)
        offset_across = jnp.clip(2 * (zz - z) + 2 * xl - 1, -1, 1) * NEW_DEV
        fresh = jnp.exp2(scores[:, 0:NEW_DEV] * SCALE)
        fresh = jnp.concatenate(
            [
                jnp.where(lead >= offset_own, fresh[0:ROWS], 0.0),
                jnp.where(lead >= offset_across, fresh[ROWS:], 0.0),
            ],
            axis=0,
        )
        old = jnp.exp2(scores[:, NEW_DEV:] * SCALE + bias[j, 0:1, 0:CACHE_DEV])
        weights = jnp.concatenate(
            [fresh.astype(jnp.bfloat16), old.astype(jnp.bfloat16)], axis=1
        )
        extended = jnp.concatenate([values, jnp.ones((KEYS, HD), jnp.bfloat16)], axis=1)
        acc[...] += jnp.dot(weights, extended, preferred_element_type=jnp.float32)

    def num_copy(h):
        return remote(num_send.at[h], num_recv.at[h], num_s.at[h], num_r.at[h], across)

    def den_copy(h):
        return remote(den_send.at[h], den_recv.at[h], den_s.at[h], den_r.at[h], across)

    def att_copy(h, off):
        e = peer(off)
        return remote(
            att_send.at[h, e],
            att_recv.at[h, expert],
            att_s.at[h, off],
            att_r.at[h, off],
            at_expert(e),
        )

    def att_local(h):
        return pltpu.make_async_copy(
            att_send.at[h, expert], att_recv.at[h, expert], local_sem.at[8 + h]
        )

    def finish(h):
        num_copy(h).wait_recv()
        den_copy(h).wait_recv()
        den_there = jnp.broadcast_to(den_recv[h][0:1, :], (HD, ROWS)).T
        numerator = own_part[h, :, 0:HD] + num_recv[h].astype(jnp.float32)
        denominator = own_part[h, :, HD:] + den_there
        attended = (numerator / denominator).astype(jnp.bfloat16)
        spread = jnp.dot(spread_q[...], attended, preferred_element_type=jnp.float32)
        att_send[h] = spread.astype(jnp.bfloat16).reshape(EXPERTS, CAP, HD)
        for off in range(1, 8):
            att_copy(h, off).start()
        att_local(h).start()

    def one_head(h, _):
        for way in range(2):
            kv_forward(h, way).wait_recv()
            kv_share(h, 2 + way).start()
        qx_copy(h).wait_recv()
        acc[...] = jnp.zeros_like(acc)

        def first(zz, _):
            block(h, zz, c)
            return 0

        lax.fori_loop(0, NZ, first, 0)
        kv_own_copy(h, 2).wait_recv()
        for which in range(4):
            kv_share(h, which).wait_recv()

        def second(zz, _):
            block(h, zz, 1 - c)
            return 0

        lax.fori_loop(0, NZ, second, 0)
        own_part[h] = acc[0:ROWS]
        num_send[h] = acc[ROWS:, 0:HD].astype(jnp.bfloat16)
        den_send[h] = acc[ROWS:, HD:].T[0:8, :]
        num_copy(h).start()
        den_copy(h).start()

        @pl.when(h >= 2)
        def _():
            finish(h - 2)

        return 0

    lax.fori_loop(0, KVH, one_head, 0)
    finish(KVH - 2)
    finish(KVH - 1)

    load_wo.wait()

    def wait_att(h, _):
        for off in range(1, 8):
            att_copy(h, off).wait_recv()
        att_local(h).wait()
        return 0

    lax.fori_loop(0, KVH, wait_att, 0)

    def exp_copy(n, off):
        r = peer(off)
        return remote(
            exp_send.at[n, r],
            exp_recv.at[n, expert],
            exp_s.at[n, off],
            exp_r.at[n, off],
            at_expert(r),
        )

    def exp_local(n):
        return pltpu.make_async_copy(
            exp_send.at[n, expert], exp_recv.at[n, expert], local_sem.at[16 + n]
        )

    arrived = jnp.concatenate([att_recv[h].reshape(SLOTS, HD) for h in range(KVH)], axis=1)

    def project_out(n, _):
        part = jnp.dot(
            arrived,
            wo[:, pl.ds(pl.multiple_of(n * NW, NW), NW)],
            preferred_element_type=jnp.float32,
        )
        exp_send[n] = part.astype(jnp.bfloat16).reshape(EXPERTS, CAP, NW)
        for off in range(1, 8):
            exp_copy(n, off).start()
        exp_local(n).start()
        return 0

    lax.fori_loop(0, NC, project_out, 0)

    def combine(n, _):
        for off in range(1, 8):
            exp_copy(n, off).wait_recv()
        exp_local(n).wait()
        back = exp_recv[n].reshape(SLOTS, NW)
        columns = pl.ds(pl.multiple_of(n * NW, NW), NW)
        mixed = jnp.dot(gates[:, 0:SLOTS], back, preferred_element_type=jnp.float32)
        mixed += jnp.dot(gates[:, SLOTS:], back, preferred_element_type=jnp.float32)
        out[:, columns] = (tokens[:, columns].astype(jnp.float32) + mixed).astype(jnp.bfloat16)
        return 0

    lax.fori_loop(0, NC, combine, 0)

    def drain_rows(k, _):
        for off in range(1, 8):
            rows_copy(k, off).wait_send()
            exp_copy(k, off).wait_send()
        return 0

    lax.fori_loop(0, KC, drain_rows, 0)

    def drain_heads(h, _):
        for way in range(3):
            kv_own_copy(h, way).wait_send()
        for way in range(2):
            kv_forward(h, way).wait_send()
        for which in range(4):
            kv_share(h, which).wait_send()
        qx_copy(h).wait_send()
        num_copy(h).wait_send()
        den_copy(h).wait_send()
        for off in range(1, 8):
            att_copy(h, off).wait_send()
        return 0

    lax.fori_loop(0, KVH, drain_heads, 0)
    for off in range(1, 8):
        bias_copy(off).wait_send()
        q_copy(off).wait_send()


def layer(kv_own, bias_own, rows_send, gather_q, spread_q, gates, cosine, sine, tokens, wq, wo):
    bf = jnp.bfloat16
    f32 = jnp.float32
    anywhere = pl.BlockSpec(memory_space=pl.ANY)
    inside = pl.BlockSpec(memory_space=pltpu.VMEM)
    dma = pltpu.SemaphoreType.DMA
    return pl.pallas_call(
        kernel,
        out_shape=jax.ShapeDtypeStruct((NEW_DEV, D), bf),
        in_specs=[anywhere, inside, anywhere] + [inside] * 6 + [anywhere] * 2,
        out_specs=inside,
        scratch_shapes=[
            pltpu.VMEM((KVH, 2 * NZ, KEYS, 2 * HD), bf),
            pltpu.VMEM((2 * NZ, 8, 384), f32),
            pltpu.VMEM((KC, EXPERTS, CAP, KW), bf),
            pltpu.VMEM((D, KVW), bf),
            pltpu.VMEM((KVW, D), bf),
            pltpu.VMEM((SLOTS, KVW), f32),
            pltpu.VMEM((EXPERTS, CAP, KVW), bf),
            pltpu.VMEM((EXPERTS, CAP, KVW), bf),
            pltpu.VMEM((KVH, 2 * ROWS, HD), bf),
            pltpu.VMEM((2 * ROWS, 2 * HD), f32),
            pltpu.VMEM((KVH, ROWS, 2 * HD), f32),
            pltpu.VMEM((KVH, ROWS, HD), bf),
            pltpu.VMEM((KVH, ROWS, HD), bf),
            pltpu.VMEM((KVH, 8, ROWS), f32),
            pltpu.VMEM((KVH, 8, ROWS), f32),
            pltpu.VMEM((KVH, EXPERTS, CAP, HD), bf),
            pltpu.VMEM((KVH, EXPERTS, CAP, HD), bf),
            pltpu.VMEM((NC, EXPERTS, CAP, NW), bf),
            pltpu.VMEM((NC, EXPERTS, CAP, NW), bf),
            dma((20,)),
            dma((KC, 8)),
            dma((KC, 8)),
            dma((8,)),
            dma((8,)),
            dma((KVH, 9)),
            dma((KVH, 9)),
            dma((8,)),
            dma((8,)),
            dma((KVH,)),
            dma((KVH,)),
            dma((KVH,)),
            dma((KVH,)),
            dma((KVH,)),
            dma((KVH,)),
            dma((KVH, 8)),
            dma((KVH, 8)),
            dma((NC, 8)),
            dma((NC, 8)),
        ],
        compiler_params=pltpu.CompilerParams(
            collective_id=0, has_side_effects=True, vmem_limit_bytes=60 * 1024 * 1024
        ),
        name="layer",
    )(kv_own, bias_own, rows_send, gather_q, spread_q, gates, cosine, sine, tokens, wq, wo)


def shards(
    new_tokens,
    norm_gain,
    router_weight,
    att_choice,
    w_query,
    w_key,
    w_value,
    w_out,
    cache_keys,
    cache_values,
    hidden_held,
    recompute_ids,
    block_live,
    cached_len,
):
    bf = jnp.bfloat16
    f32 = jnp.float32
    blk_index = lax.axis_index("blk")
    length = cached_len[0]
    tokens = new_tokens[0]
    normed = normalize(tokens, norm_gain)
    held_norm = normalize(hidden_held[0], norm_gain)
    new_pos = length + blk_index * NEW_DEV + jnp.arange(NEW_DEV, dtype=jnp.int32)
    held_start = recompute_ids[0, 0] * CB
    held_pos = blk_index * CACHE_DEV + held_start + jnp.arange(CB, dtype=jnp.int32)
    both_rows = jnp.concatenate([normed, held_norm], axis=0)
    cosine, sine = rope_tables(jnp.concatenate([new_pos, held_pos]))
    key_proj = rotate(
        jnp.dot(both_rows, w_key, preferred_element_type=f32), cosine, sine
    ).astype(bf)
    value_proj = (
        jnp.dot(both_rows, w_value, preferred_element_type=f32).astype(bf).reshape(-1, KVH, HD)
    )
    fresh = jnp.concatenate([key_proj, value_proj], axis=-1).transpose(1, 0, 2)
    cached = jnp.concatenate(
        [cache_keys[0].reshape(-1, KVH, HD), cache_values[0].reshape(-1, KVH, HD)], axis=-1
    ).transpose(1, 0, 2)
    kv_own = jnp.concatenate([fresh[:, :NEW_DEV], cached], axis=1)
    kv_own = lax.dynamic_update_slice(
        kv_own, fresh[:, NEW_DEV:], (0, NEW_DEV + held_start, 0)
    )
    slot_pos = blk_index * CACHE_DEV + jnp.arange(CACHE_DEV, dtype=jnp.int32)
    usable = (slot_pos < length) & (jnp.repeat(block_live[0], CB) == 1)
    bias_own = jnp.where(usable, 0.0, MASKED).astype(f32)
    bias_own = jnp.broadcast_to(jnp.pad(bias_own, (0, 384 - CACHE_DEV))[None], (8, 384))

    logits = jnp.dot(normed, router_weight, preferred_element_type=f32)
    picked = att_choice[0]
    ids = jnp.arange(EXPERTS, dtype=jnp.int32)
    one_hot = picked.T.reshape(-1)[:, None] == ids[None, :]
    chosen = jnp.sum(jnp.where(one_hot, jnp.concatenate([logits, logits], 0), 0.0), axis=1)
    gate_first = jax.nn.sigmoid(chosen[:NEW_DEV] - chosen[NEW_DEV:])
    order = jnp.arange(ROWS, dtype=jnp.int32)
    earlier = (order[:, None] > order[None, :]).astype(bf)
    before = jnp.dot(earlier, one_hot.astype(bf), preferred_element_type=f32)
    slot = jnp.sum(jnp.where(one_hot, before, 0.0), axis=1).astype(jnp.int32)
    target = picked.T.reshape(-1) * CAP + slot
    slots = jnp.arange(SLOTS, dtype=jnp.int32)
    gather_q = (target[:, None] == slots[None, :]).astype(bf)
    spread_q = (slots[:, None] == target[None, :]).astype(bf)
    spread = spread_q[:, :NEW_DEV] + spread_q[:, NEW_DEV:]
    rows_send = jnp.dot(spread, normed, preferred_element_type=f32).astype(bf)
    both_gates = jnp.where(
        target[:NEW_DEV, None] == slots[None, :], gate_first[:, None], 0.0
    ) + jnp.where(target[NEW_DEV:, None] == slots[None, :], 1.0 - gate_first[:, None], 0.0)
    gates_high = both_gates.astype(bf)
    gates_low = (both_gates - gates_high.astype(f32)).astype(bf)
    gates = jnp.concatenate([gates_high, gates_low], axis=1)
    q_cos = jnp.concatenate([cosine[:NEW_DEV]] * 2, 0)
    q_sin = jnp.concatenate([sine[:NEW_DEV]] * 2, 0)
    mixed = layer(
        kv_own,
        bias_own,
        rows_send.reshape(EXPERTS, CAP, D),
        gather_q,
        spread_q,
        gates,
        q_cos,
        q_sin,
        tokens,
        w_query[0],
        w_out[0],
    )
    return mixed[None]


def solution(mesh):
    placed = (
        P("expert", "blk", None),
        P(),
        P(),
        P("expert", "blk", None),
        P("expert", None, None),
        P(),
        P(),
        P("expert", None, None),
        P("expert", "blk", None),
        P("expert", "blk", None),
        P("expert", "blk", None),
        P("expert", "blk"),
        P("expert", "blk"),
        P("expert"),
    )
    return jax.shard_map(
        shards, mesh=mesh, in_specs=placed, out_specs=P("expert", "blk", None), check_vma=False
    )
```

time: 331 us -> 159 us (0.48)
  Pallas kernels: 0 us -> 135 us
  blocking collectives: 109 us -> 0 us
  local copies, waits for them, and re-layouts: 64.6 us -> 7.96 us
  waiting for transfers between devices: 48.3 us -> 0 us
  matrix products: 54 us -> 6.42 us
  starting transfers between devices: 22.6 us -> 0 us
  between operations: 15.8 us -> 1.66 us
  other arithmetic: 14.7 us -> 7.14 us
    pallas_call x0 -> x1, Pallas kernels: none -> 135 us  [layer(): pl.pallas_call(kernel, out_shape=jax.ShapeDtypeStruct((NEW_DEV, D), bf),...]
    unnamed x1 -> x0, blocking collectives: 88.5 us -> none
    all_to_all x4 -> x0, waiting for transfers between devices: 48.2 us -> none  [the longest x1 23.6 us: shards(): lax.all_to_all(projected.astype(jnp.bfloat16).reshape(sources, slot_count...]
    dot_general x7 -> x5, matrix products: 54 us -> 6.42 us  [the longest x1 3.03 us: shards(): jnp.dot(both_rows, w_key, preferred_element_type=f32)]
    all_gather x2 -> x0, local copies, waits for them, and re-layouts: 37.3 us -> none  [the longest x1 18.9 us: shards(): piece_keys = lax.all_gather(local_keys, 'blk', axis=0, tiled=True)]
    all_to_all x4 -> x0, starting transfers between devices: 22.5 us -> none  [the longest x1 7.29 us: shards(): lax.all_to_all(turned, 'expert', split_axis=0, concat_axis=0, tiled=True)]
    all_to_all x1 -> x0, blocking collectives: 20.3 us -> none  [shards(): lax.all_to_all(send_out.reshape(experts, capacity, key_width), 'expert',...]
    scatter x3 -> x0, local copies, waits for them, and re-layouts: 7 us -> none  [the longest x1 3.69 us: shards(): send_rows = jnp.zeros((experts * capacity, tokens.shape[1]), jnp.bfloat16...]
  transfers between devices with their start and end apart: 6 -> 0, of which waited for: 3 -> 0; matrix products, arithmetic and copies ran while one was open for 22% -> 0% of each run, Pallas kernels for 0% -> 0%
where the time goes in v1:
time: 159 us; the launch traced here: 158 us
  Pallas kernels  135 us (85%)
  local copies, waits for them, and re-layouts  7.96 us (5%)
  other arithmetic  7.14 us (4%)
  matrix products  6.42 us (4%)
  between operations  1.66 us (1%)
    pallas_call x1, Pallas kernels, layer(): pl.pallas_call(kernel, out_shape=jax.ShapeDtypeStruct((NEW_DEV, D), bf),...  135 us
    unnamed x25, local copies, waits for them, and re-layouts  4.96 us

profile of v1, /device:TPU:0, one launch (start us, length us, event | category | flops | bytes accessed | tf_op | source)
XLA Modules:
  0.0 158.1 jit_solution(10570543212103051750)
XLA Ops:
  0.0 0.0 copy-start
  1.4 0.4 multiply_cosine_fusion
  1.8 0.1 pad_maximum_fusion.7
  1.9 1.2 fusion.2
  3.1 1.3 fusion.4
  4.4 0.0 copy-done.6
  4.4 0.1 fusion.9
  4.6 0.1 fusion.11
  4.7 3.0 %convolution_bitcast_fusion = f32[20,8,8,128]{3,2,1,0:T(8,128)S(1)} fusion(bf16[2048,1024]{1,0:T(8,128)(2,1)} %param.19, bf16[32,2048]{1,0:T(8,128)(2,1)S(1)} %fusion.11, bf16[128,2048]{1,0:T(8,128)(2,1)S(1)} %fusion.4), kind=kOutput, calls=%fused_computation.5 | convolution fusion | flops 672399360 | bytes 5505024 | tf_op jit(solution)/shard_map/dot_general | solution.py:583
  7.8 0.0 copy-start.9
  7.8 0.2 fusion.23
  8.0 0.3 fusion.6
  8.3 1.7 %copy-done.9 = bf16[2048,1024]{1,0:T(8,128)(2,1)S(1)} copy-done((bf16[2048,1024]{1,0:T(8,128)(2,1)S(1)}, bf16[2048,1024]{1,0:T(8,128)(2,1)}, u32[]{:S(2)}) %copy-start.9) | copy-done | bytes 4194328
  9.9 0.9 fusion
  10.9 0.0 copy-start.4
  10.9 0.1 copy.30
  10.9 0.1 maximum_bitcast_fusion.1
  11.0 0.0 copy-start.5
  11.0 1.0 copy-done.4
  12.0 0.1 copy.23
  12.1 0.1 copy.19
  12.2 0.2 copy-done.5
  12.4 0.1 copy.24
  12.5 0.0 slice-start
  12.5 0.1 copy.20
  12.6 0.2 maximum_bitcast_fusion
  12.8 0.8 slice-done
  13.6 0.1 pad_maximum_fusion
  13.7 0.9 slice_dynamic-update-slice_fusion.kv_own
  14.7 0.2 fusion.25
  15.0 0.2 fusion.1
  15.2 0.1 fusion.12
  15.3 0.8 pad_maximum_fusion.4.gates
  16.1 0.1 fusion.14
  16.2 0.0 copy-start.10
  16.2 0.7 pad_maximum_fusion.5.cosine
  16.9 0.7 pad_maximum_fusion.6.sine
  17.5 0.1 fusion.7.spread_q
  17.6 0.0 copy-start.3
  17.6 2.0 %convolution_convert_fusion = bf16[512,2048]{1,0:T(8,128)(2,1)} fusion(bf16[128,2048]{1,0:T(8,128)(2,1)S(1)} %fusion.4, bf16[512,256]{1,0:T(8,128)(2,1)S(1)} %fusion.7.spread_q), kind=kOutput, calls=%fused_computation | convolution fusion | flops 269549568 | bytes 2883584 | tf_op jit(solution)/shard_map/dot_general | solution.py:616
  19.7 0.0 copy-done.1
  19.7 0.8 fusion.8.gather_q
  20.5 0.0 copy-done.10
  20.5 0.1 broadcast_in_dim.37
  20.6 0.1 eq.81
  20.7 0.6 broadcast_in_dim.40.bias_own
  21.3 134.9 %layer.1 = bf16[128,2048]{1,0:T(8,128)(2,1)} custom-call(bf16[8,448,256]{2,1,0:T(8,128)(2,1)} %copy-done.1, f32[8,384]{1,0:T(8,128)} %broadcast_in_dim.40.bias_own, bf16[8,64,2048]{2,1,0:T(8,128)(2,1)} %bitcast.50, bf16[256,512]{1,0:T(8,128)(2,1)} %fusion.8.gather_q, bf16[512,256]{1,0:T(8,128)(2,1)} %copy-done.3, bf16[128,1024]{1,0:T(8,128)(2,1)} %pad_maximum_fusion.4.gates, ...), custom_call_target="tpu_custom_call" | custom-call | tf_op jit(solution)/shard_map/layer/pallas_call | solution.py:502
  156.2 1.9 %copy.35 = bf16[1,128,2048]{2,1,0:T(8,128)(2,1)} copy(bf16[1,128,2048]{2,1,0:T(8,128)(2,1)} %bitcast.57) | data formatting | bytes 1048576
  (24 shorter events, 0.2 us)
Async XLA Ops:
  0.0 14.6 %copy-start = (bf16[2048,8]{0,1:T(8,128)(2,1)S(1)}, bf16[2048,8]{0,1:T(8,128)(2,1)}, u32[]{:S(2)}) copy-start(bf16[2048,8]{0,1:T(8,128)(2,1)} %param.16) | copy-start | bytes 98308
  0.0 4.5 %copy-start.7 = (f32[2048]{0:T(1024)S(1)}, f32[2048]{0:T(1024)}, u32[]{:S(2)}) copy-start(f32[2048]{0:T(1024)} %param.15) | copy-start | bytes 24580
  0.0 4.4 %copy-start.6 = (bf16[1,32,2048]{2,1,0:T(8,128)(2,1)S(1)}, bf16[1,32,2048]{2,1,0:T(8,128)(2,1)}, u32[]{:S(2)}) copy-start(bf16[1,32,2048]{2,1,0:T(8,128)(2,1)} %param.24) | copy-start | bytes 393220
  7.8 2.2 %copy-start.9 = (bf16[2048,1024]{1,0:T(8,128)(2,1)S(1)}, bf16[2048,1024]{1,0:T(8,128)(2,1)}, u32[]{:S(2)}) copy-start(bf16[2048,1024]{1,0:T(8,128)(2,1)} %param.20) | copy-start | bytes 12582916
  10.9 1.1 copy-start.4
  11.0 1.2 copy-start.2
  11.0 1.4 copy-start.5
  12.5 1.0 slice-start
  13.6 1.3 copy-start.8
  14.7 5.0 %copy-start.1 = (bf16[8,448,256]{2,1,0:T(8,128)(2,1)}, bf16[8,448,256]{2,1,0:T(8,128)(2,1)S(1)}, u32[]{:S(2)}) copy-start(bf16[8,448,256]{2,1,0:T(8,128)(2,1)S(1)} %slice_dynamic-update-slice_fusion.kv_own) | copy-start | bytes 5505028
  16.2 4.3 %copy-start.10 = (s32[1,10]{1,0:T(1,128)S(1)}, s32[1,10]{1,0:T(1,128)}, u32[]{:S(2)}) copy-start(s32[1,10]{1,0:T(1,128)} %param.26) | copy-start | bytes 124
  17.6 3.7 %copy-start.3 = (bf16[512,256]{1,0:T(8,128)(2,1)}, bf16[512,256]{1,0:T(8,128)(2,1)S(1)}, u32[]{:S(2)}) copy-start(bf16[512,256]{1,0:T(8,128)(2,1)S(1)} %fusion.7.spread_q) | copy-start | bytes 786436

commit v2 on v1

--- a/solution.py
+++ b/solution.py
@@ -57,6 +57,12 @@
     v = projected.reshape(row_count, KVH, HD)
     swapped = jnp.concatenate([v[..., half_width:], v[..., :half_width]], axis=-1)
     return v * cosine[:, None, :] + swapped * sine[:, None, :]
+
+
+def product_nt(left, right):
+    return lax.dot_general(
+        left, right, (((1,), (1,)), ((), ())), preferred_element_type=jnp.float32
+    )
 
 
 def kernel(
@@ -316,29 +322,38 @@
         - lax.broadcasted_iota(jnp.int32, (ROWS, NEW_DEV), 1)
     )
 
-    def block(h, zz, cc):
-        j = zz * 2 + cc
-        keys = kv[h, j, :, 0:HD]
-        values = kv[h, j, :, HD : 2 * HD]
-        scores = lax.dot_general(
-            queries[h], keys, (((1,), (1,)), ((), ())), preferred_element_type=jnp.float32
-        )
-        offset_own = jnp.clip((j - mine) * NEW_DEV, -NEW_DEV, NEW_DEV)
-        offset_across = jnp.clip(2 * (zz - z) + 2 * xl - 1, -1, 1) * NEW_DEV
-        fresh = jnp.exp2(scores[:, 0:NEW_DEV] * SCALE)
-        fresh = jnp.concatenate(
-            [
-                jnp.where(lead >= offset_own, fresh[0:ROWS], 0.0),
-                jnp.where(lead >= offset_across, fresh[ROWS:], 0.0),
-            ],
+    def half(h, cc):
+        old_part = slice(NEW_DEV, KEYS)
+        blocks = [zz * 2 + cc for zz in range(NZ)]
+        new_keys = jnp.concatenate([kv[h, j, 0:NEW_DEV, 0:HD] for j in blocks], axis=0)
+        old_keys = jnp.concatenate([kv[h, j, old_part, 0:HD] for j in blocks], axis=0)
+        new_scores = product_nt(queries[h], new_keys)
+        old_scores = product_nt(queries[h], old_keys)
+        shut = jnp.concatenate([bias[j, 0:1, 0:CACHE_DEV] for j in blocks], axis=1)
+        pieces = []
+        for zz, j in enumerate(blocks):
+            offset_own = jnp.clip((j - mine) * NEW_DEV, -NEW_DEV, NEW_DEV)
+            offset_across = jnp.clip(2 * (zz - z) + 2 * xl - 1, -1, 1) * NEW_DEV
+            fresh = jnp.exp2(new_scores[:, zz * NEW_DEV : (zz + 1) * NEW_DEV] * SCALE)
+            pieces.append(
+                jnp.concatenate(
+                    [
+                        jnp.where(lead >= offset_own, fresh[0:ROWS], 0.0),
+                        jnp.where(lead >= offset_across, fresh[ROWS:], 0.0),
+                    ],
+                    axis=0,
+                ).astype(jnp.bfloat16)
+            )
+        pieces.append(jnp.exp2(old_scores * SCALE + shut).astype(jnp.bfloat16))
+        values = jnp.concatenate(
+            [kv[h, j, 0:NEW_DEV, HD : 2 * HD] for j in blocks]
+            + [kv[h, j, old_part, HD : 2 * HD] for j in blocks],
             axis=0,
         )
-        old = jnp.exp2(scores[:, NEW_DEV:] * SCALE + bias[j, 0:1, 0:CACHE_DEV])
-        weights = jnp.concatenate(
-            [fresh.astype(jnp.bfloat16), old.astype(jnp.bfloat16)], axis=1
-        )
-        extended = jnp.concatenate([values, jnp.ones((KEYS, HD), jnp.bfloat16)], axis=1)
-        acc[...] += jnp.dot(weights, extended, preferred_element_type=jnp.float32)
+        extended = jnp.concatenate([values, jnp.ones((NZ * KEYS, HD), jnp.bfloat16)], axis=1)
+        return jnp.dot(
+            jnp.concatenate(pieces, axis=1), extended, preferred_element_type=jnp.float32
+        )
 
     def num_copy(h):
         return remote(num_send.at[h], num_recv.at[h], num_s.at[h], num_r.at[h], across)
@@ -379,22 +394,27 @@
             kv_forward(h, way).wait_recv()
             kv_share(h, 2 + way).start()
         qx_copy(h).wait_recv()
-        acc[...] = jnp.zeros_like(acc)
-
-        def first(zz, _):
-            block(h, zz, c)
+
+        def side(i, _):
+            @pl.when(i == 1)
+            def _():
+                kv_own_copy(h, 2).wait_recv()
+                for which in range(4):
+                    kv_share(h, which).wait_recv()
+
+            part = half(h, (c + i) % 2)
+
+            @pl.when(i == 0)
+            def _():
+                acc[...] = part
+
+            @pl.when(i == 1)
+            def _():
+                acc[...] += part
+
             return 0
 
-        lax.fori_loop(0, NZ, first, 0)
-        kv_own_copy(h, 2).wait_recv()
-        for which in range(4):
-            kv_share(h, which).wait_recv()
-
-        def second(zz, _):
-            block(h, zz, 1 - c)
-            return 0
-
-        lax.fori_loop(0, NZ, second, 0)
+        lax.fori_loop(0, 2, side, 0)
         own_part[h] = acc[0:ROWS]
         num_send[h] = acc[ROWS:, 0:HD].astype(jnp.bfloat16)
         den_send[h] = acc[ROWS:, HD:].T[0:8, :]

time: 159 us -> 146 us (0.918)
  Pallas kernels: 135 us -> 122 us
    pallas_call x1, Pallas kernels: 135 us -> 122 us  [layer(): pl.pallas_call(kernel, out_shape=jax.ShapeDtypeStruct((NEW_DEV, D), bf),...]
where the time goes in v2:
time: 146 us; the launch traced here: 145 us
  Pallas kernels  122 us (84%)
  local copies, waits for them, and re-layouts  7.96 us (5%)
  other arithmetic  7.14 us (5%)
  matrix products  6.42 us (4%)
  between operations  1.66 us (1%)
    pallas_call x1, Pallas kernels, layer(): pl.pallas_call(kernel, out_shape=jax.ShapeDtypeStruct((NEW_DEV, D), bf),...  122 us
    unnamed x25, local copies, waits for them, and re-layouts  4.96 us
    dot_general x1, matrix products, shards(): jnp.dot(both_rows, w_key, preferred_element_type=f32)  3.03 us

profile of v2, /device:TPU:0, one launch (start us, length us, event | category | flops | bytes accessed | tf_op | source)
XLA Modules:
  0.0 145.5 jit_solution(32916595378005497)
XLA Ops:
  0.0 0.0 copy-start
  1.4 0.4 multiply_cosine_fusion
  1.8 0.1 pad_maximum_fusion.7
  1.9 1.2 fusion.2
  3.1 1.3 fusion.4
  4.4 0.0 copy-done.6
  4.4 0.1 fusion.9
  4.6 0.1 fusion.11
  4.7 3.0 %convolution_bitcast_fusion = f32[20,8,8,128]{3,2,1,0:T(8,128)S(1)} fusion(bf16[2048,1024]{1,0:T(8,128)(2,1)} %param.19, bf16[32,2048]{1,0:T(8,128)(2,1)S(1)} %fusion.11, bf16[128,2048]{1,0:T(8,128)(2,1)S(1)} %fusion.4), kind=kOutput, calls=%fused_computation.5 | convolution fusion | flops 672399360 | bytes 5505024 | tf_op jit(solution)/shard_map/dot_general | solution.py:603
  7.8 0.0 copy-start.9
  7.8 0.2 fusion.23
  8.0 0.3 fusion.6
  8.3 1.7 %copy-done.9 = bf16[2048,1024]{1,0:T(8,128)(2,1)S(1)} copy-done((bf16[2048,1024]{1,0:T(8,128)(2,1)S(1)}, bf16[2048,1024]{1,0:T(8,128)(2,1)}, u32[]{:S(2)}) %copy-start.9) | copy-done | bytes 4194328
  9.9 0.9 fusion
  10.9 0.0 copy-start.4
  10.9 0.1 copy.30
  10.9 0.1 maximum_bitcast_fusion.1
  11.0 0.0 copy-start.5
  11.0 1.0 copy-done.4
  12.0 0.1 copy.23
  12.1 0.1 copy.19
  12.2 0.2 copy-done.5
  12.4 0.1 copy.24
  12.5 0.0 slice-start
  12.5 0.1 copy.20
  12.6 0.2 maximum_bitcast_fusion
  12.8 0.8 slice-done
  13.6 0.1 pad_maximum_fusion
  13.7 0.9 slice_dynamic-update-slice_fusion.kv_own
  14.7 0.2 fusion.25
  15.0 0.2 fusion.1
  15.2 0.1 fusion.12
  15.3 0.8 pad_maximum_fusion.4.gates
  16.1 0.1 fusion.14
  16.2 0.0 copy-start.10
  16.2 0.7 pad_maximum_fusion.5.cosine
  16.9 0.7 pad_maximum_fusion.6.sine
  17.5 0.1 fusion.7.spread_q
  17.6 0.0 copy-start.3
  17.6 2.0 %convolution_convert_fusion = bf16[512,2048]{1,0:T(8,128)(2,1)} fusion(bf16[128,2048]{1,0:T(8,128)(2,1)S(1)} %fusion.4, bf16[512,256]{1,0:T(8,128)(2,1)S(1)} %fusion.7.spread_q), kind=kOutput, calls=%fused_computation | convolution fusion | flops 269549568 | bytes 2883584 | tf_op jit(solution)/shard_map/dot_general | solution.py:636
  19.7 0.0 copy-done.1
  19.7 0.8 fusion.8.gather_q
  20.5 0.0 copy-done.10
  20.5 0.1 broadcast_in_dim.37
  20.6 0.1 eq.81
  20.7 0.6 broadcast_in_dim.40.bias_own
  21.3 122.3 %layer.1 = bf16[128,2048]{1,0:T(8,128)(2,1)} custom-call(bf16[8,448,256]{2,1,0:T(8,128)(2,1)} %copy-done.1, f32[8,384]{1,0:T(8,128)} %broadcast_in_dim.40.bias_own, bf16[8,64,2048]{2,1,0:T(8,128)(2,1)} %bitcast.50, bf16[256,512]{1,0:T(8,128)(2,1)} %fusion.8.gather_q, bf16[512,256]{1,0:T(8,128)(2,1)} %copy-done.3, bf16[128,1024]{1,0:T(8,128)(2,1)} %pad_maximum_fusion.4.gates, ...), custom_call_target="tpu_custom_call" | custom-call | tf_op jit(solution)/shard_map/layer/pallas_call | solution.py:522
  143.6 1.9 %copy.35 = bf16[1,128,2048]{2,1,0:T(8,128)(2,1)} copy(bf16[1,128,2048]{2,1,0:T(8,128)(2,1)} %bitcast.57) | data formatting | bytes 1048576
  (24 shorter events, 0.2 us)
Async XLA Ops:
  0.0 14.6 %copy-start = (bf16[2048,8]{0,1:T(8,128)(2,1)S(1)}, bf16[2048,8]{0,1:T(8,128)(2,1)}, u32[]{:S(2)}) copy-start(bf16[2048,8]{0,1:T(8,128)(2,1)} %param.16) | copy-start | bytes 98308
  0.0 4.5 %copy-start.7 = (f32[2048]{0:T(1024)S(1)}, f32[2048]{0:T(1024)}, u32[]{:S(2)}) copy-start(f32[2048]{0:T(1024)} %param.15) | copy-start | bytes 24580
  0.0 4.4 %copy-start.6 = (bf16[1,32,2048]{2,1,0:T(8,128)(2,1)S(1)}, bf16[1,32,2048]{2,1,0:T(8,128)(2,1)}, u32[]{:S(2)}) copy-start(bf16[1,32,2048]{2,1,0:T(8,128)(2,1)} %param.24) | copy-start | bytes 393220
  7.8 2.2 %copy-start.9 = (bf16[2048,1024]{1,0:T(8,128)(2,1)S(1)}, bf16[2048,1024]{1,0:T(8,128)(2,1)}, u32[]{:S(2)}) copy-start(bf16[2048,1024]{1,0:T(8,128)(2,1)} %param.20) | copy-start | bytes 12582916
  10.9 1.1 copy-start.4
  11.0 1.2 copy-start.2
  11.0 1.4 copy-start.5
  12.5 1.0 slice-start
  13.6 1.3 copy-start.8
  14.7 5.0 %copy-start.1 = (bf16[8,448,256]{2,1,0:T(8,128)(2,1)}, bf16[8,448,256]{2,1,0:T(8,128)(2,1)S(1)}, u32[]{:S(2)}) copy-start(bf16[8,448,256]{2,1,0:T(8,128)(2,1)S(1)} %slice_dynamic-update-slice_fusion.kv_own) | copy-start | bytes 5505028
  16.2 4.3 %copy-start.10 = (s32[1,10]{1,0:T(1,128)S(1)}, s32[1,10]{1,0:T(1,128)}, u32[]{:S(2)}) copy-start(s32[1,10]{1,0:T(1,128)} %param.26) | copy-start | bytes 124
  17.6 3.7 %copy-start.3 = (bf16[512,256]{1,0:T(8,128)(2,1)}, bf16[512,256]{1,0:T(8,128)(2,1)S(1)}, u32[]{:S(2)}) copy-start(bf16[512,256]{1,0:T(8,128)(2,1)S(1)} %fusion.7.spread_q) | copy-start | bytes 786436

commit v3 on v2

--- a/solution.py
+++ b/solution.py
@@ -1,8 +1,8 @@
-import functools
 import math
 
 import jax
 import jax.numpy as jnp
+import numpy as np
 from jax import lax
 from jax.experimental import pallas as pl
 from jax.experimental.pallas import tpu as pltpu
@@ -26,6 +26,10 @@
 NC = 4
 NW = D // NC
 NZ = 4
+PAIRS = 4
+PAIR = 2 * HD
+BLK_DEV = 10
+BIAS_WIDTH = 384
 
 epsilon = 1e-06
 theta_base = 10000.0
@@ -34,31 +38,6 @@
 SCALE = LOG2E / math.sqrt(HD)
 
 
-def normalize(hidden, norm_gain):
-    widened = hidden.astype(jnp.float32)
-    inverse = lax.rsqrt(jnp.mean(widened * widened, axis=-1, keepdims=True) + epsilon)
-    return (widened * inverse * norm_gain).astype(jnp.bfloat16)
-
-
-def rope_tables(positions):
-    half_width = HD // 2
-    frequency = jnp.exp(
-        jnp.arange(half_width, dtype=jnp.float32) * (-math.log(theta_base) / half_width)
-    )
-    angles = positions.astype(jnp.float32)[:, None] * frequency[None, :]
-    cosine = jnp.cos(angles)
-    sine = jnp.sin(angles)
-    return jnp.concatenate([cosine, cosine], 1), jnp.concatenate([-sine, sine], 1)
-
-
-def rotate(projected, cosine, sine):
-    row_count = projected.shape[0]
-    half_width = HD // 2
-    v = projected.reshape(row_count, KVH, HD)
-    swapped = jnp.concatenate([v[..., half_width:], v[..., :half_width]], axis=-1)
-    return v * cosine[:, None, :] + swapped * sine[:, None, :]
-
-
 def product_nt(left, right):
     return lax.dot_general(
         left, right, (((1,), (1,)), ((), ())), preferred_element_type=jnp.float32
@@ -66,15 +45,20 @@
 
 
 def kernel(
-    kv_own,
-    bias_own,
-    rows_send,
-    gather_q,
-    spread_q,
-    gates,
-    cosine,
-    sine,
+    length_ref,
+    held_ref,
+    live_ref,
     tokens,
+    hidden,
+    gain,
+    choice,
+    router,
+    base,
+    step,
+    w_key,
+    w_value,
+    cache_keys,
+    cache_values,
     w_query,
     w_out,
     out,
@@ -97,6 +81,18 @@
     att_recv,
     exp_send,
     exp_recv,
+    wk,
+    wv,
+    old_k,
+    old_v,
+    both,
+    rows_send,
+    bias_own,
+    gather_q,
+    spread_q,
+    gates,
+    cosine,
+    sine,
     local_sem,
     rows_s,
     rows_r,
@@ -168,16 +164,71 @@
 
     load_wq = pltpu.make_async_copy(w_query, wq, local_sem.at[0])
     load_wo = pltpu.make_async_copy(w_out, wo, local_sem.at[1])
-    load_kv = pltpu.make_async_copy(kv_own, kv.at[:, mine], local_sem.at[2])
+
+    def load_wk(p):
+        columns = pl.ds(p * PAIR, PAIR)
+        return pltpu.make_async_copy(w_key.at[:, columns], wk.at[p], local_sem.at[20 + p])
+
+    def load_wv(p):
+        columns = pl.ds(p * PAIR, PAIR)
+        return pltpu.make_async_copy(w_value.at[:, columns], wv.at[p], local_sem.at[24 + p])
+
+    load_old_k = pltpu.make_async_copy(cache_keys, old_k, local_sem.at[28])
+    load_old_v = pltpu.make_async_copy(cache_values, old_v, local_sem.at[29])
+    load_old_k.start()
+    load_old_v.start()
+    for p in range(PAIRS):
+        load_wk(p).start()
+        load_wv(p).start()
     load_wq.start()
-    load_kv.start()
     load_wo.start()
-    pl.semaphore_wait(barrier, 15)
+
+    def norm(hidden_rows):
+        widened = hidden_rows.astype(jnp.float32)
+        inverse = lax.rsqrt(jnp.mean(widened * widened, axis=-1, keepdims=True) + epsilon)
+        return (widened * inverse * gain[...]).astype(jnp.bfloat16)
+
+    both[0:NEW_DEV] = norm(tokens[...])
+    both[NEW_DEV:] = norm(hidden[...])
+
+    lane = lax.broadcasted_iota(jnp.int32, (NEW_DEV, HD), 1)
+    row = lax.broadcasted_iota(jnp.int32, (NEW_DEV, HD), 0)
+    earlier = (row > lane).astype(jnp.bfloat16)
+    hot = [choice[:, k : k + 1] == lane for k in range(2)]
+    count = [
+        jnp.dot(earlier, jnp.where(m, 1.0, 0.0).astype(jnp.bfloat16), preferred_element_type=jnp.float32)
+        for m in hot
+    ]
+    total = jnp.sum(jnp.where(hot[0], 1.0, 0.0), axis=0, keepdims=True)
+    count[1] = count[1] + total
+    slot_lane = lax.broadcasted_iota(jnp.int32, (NEW_DEV, SLOTS), 1)
+    at_slot = []
+    for k in range(2):
+        slot = jnp.sum(jnp.where(hot[k], count[k], 0.0), axis=1, keepdims=True)
+        target = choice[:, k : k + 1] * CAP + slot.astype(jnp.int32)
+        at_slot.append(slot_lane == target)
+    placed = [jnp.where(m, 1.0, 0.0) for m in at_slot]
+    gather_q[0:NEW_DEV] = placed[0].astype(jnp.bfloat16)
+    gather_q[NEW_DEV:] = placed[1].astype(jnp.bfloat16)
+    spread = [m.T for m in placed]
+    spread_q[:, 0:NEW_DEV] = spread[0].astype(jnp.bfloat16)
+    spread_q[:, NEW_DEV:] = spread[1].astype(jnp.bfloat16)
+    dispatch = (spread[0] + spread[1]).astype(jnp.bfloat16)
+    for k in range(KC):
+        rows_send[k] = (
+            jnp.dot(
+                dispatch,
+                both[0:NEW_DEV, k * KW : (k + 1) * KW],
+                preferred_element_type=jnp.float32,
+            )
+            .astype(jnp.bfloat16)
+            .reshape(EXPERTS, CAP, KW)
+        )
 
     def rows_copy(k, off):
         e = peer(off)
         return remote(
-            rows_send.at[e, :, pl.ds(pl.multiple_of(k * KW, KW), KW)],
+            rows_send.at[k, e],
             rows.at[k, expert],
             rows_s.at[k, off],
             rows_r.at[k, off],
@@ -186,14 +237,14 @@
 
     def rows_local(k):
         return pltpu.make_async_copy(
-            rows_send.at[expert, :, pl.ds(pl.multiple_of(k * KW, KW), KW)],
+            rows_send.at[k, expert],
             rows.at[k, expert],
             local_sem.at[3 + k],
         )
 
     def kv_own_copy(h, way):
         return remote(
-            kv_own.at[h],
+            kv.at[h, mine],
             kv.at[h, mine],
             kv_s.at[h, way],
             kv_r.at[h, way],
@@ -233,17 +284,67 @@
         rows_local(k).start()
         return 0
 
+    pl.semaphore_wait(barrier, 15)
     lax.fori_loop(0, KC, send_rows, 0)
 
-    def send_kv(h, _):
-        for way in range(3):
-            kv_own_copy(h, way).start()
-        return 0
-
-    lax.fori_loop(0, KVH, send_kv, 0)
+    cb = base[0:1, :]
+    sb = base[1:2, :]
+    ch = base[2:3, :]
+    sh = base[3:4, :]
+    ct = step[0]
+    st = step[1]
+    sign = jnp.where(lax.broadcasted_iota(jnp.int32, (1, HD), 1) < HD // 2, -1.0, 1.0)
+    cosine[0:NEW_DEV] = cb * ct - sb * st
+    sine[0:NEW_DEV] = (sb * ct + cb * st) * sign
+    cosine[NEW_DEV:] = ch * ct[0:CB] - sh * st[0:CB]
+    sine[NEW_DEV:] = (sh * ct[0:CB] + ch * st[0:CB]) * sign
+    place = lax.broadcasted_iota(jnp.int32, (8, BIAS_WIDTH), 1)
+    live = jnp.zeros((8, BIAS_WIDTH), jnp.int32)
+    for j in range(BLK_DEV):
+        live = jnp.where(place // CB == j, live_ref[0, j], live)
+    usable = (live == 1) & (blk * CACHE_DEV + place < length_ref[0])
+    bias_own[...] = jnp.where(usable, 0.0, MASKED)
+    bias[mine] = bias_own[...]
+
+    load_old_k.wait()
+    load_old_v.wait()
+    held = lax.broadcasted_iota(jnp.int32, (CACHE_DEV, HD), 0) // CB == held_ref[0, 0]
+
+    for p in range(PAIRS):
+        load_wk(p).wait()
+        load_wv(p).wait()
+        keys = jnp.dot(both[...], wk[p], preferred_element_type=jnp.float32)
+        values = jnp.dot(both[...], wv[p], preferred_element_type=jnp.float32)
+        for i in range(2):
+            h = 2 * p + i
+            k_head = keys[:, i * HD : (i + 1) * HD]
+            k_head = k_head * cosine[...] + pltpu.roll(k_head, HD // 2, 1) * sine[...]
+            v_head = values[:, i * HD : (i + 1) * HD]
+            for new, old, at in ((k_head, old_k, 0), (v_head, old_v, HD)):
+                new = new.astype(jnp.bfloat16)
+                kv[h, mine, 0:NEW_DEV, at : at + HD] = new[0:NEW_DEV]
+                kv[h, mine, NEW_DEV:, at : at + HD] = jnp.where(
+                    held,
+                    jnp.concatenate([new[NEW_DEV:]] * BLK_DEV, axis=0),
+                    old[:, h * HD : (h + 1) * HD],
+                )
+        for i in range(2):
+            for way in range(3):
+                kv_own_copy(2 * p + i, way).start()
     for off in range(1, 8):
         bias_copy(off).start()
-    bias[mine] = bias_own[...]
+
+    logits = jnp.dot(both[0:NEW_DEV], router[...], preferred_element_type=jnp.float32)
+    chosen = [
+        jnp.sum(jnp.where(m[:, 0:EXPERTS], logits, 0.0), axis=1, keepdims=True) for m in hot
+    ]
+    gate_first = jax.nn.sigmoid(chosen[0] - chosen[1])
+    both_gates = jnp.where(at_slot[0], gate_first, 0.0) + jnp.where(
+        at_slot[1], 1.0 - gate_first, 0.0
+    )
+    gates_high = both_gates.astype(jnp.bfloat16)
+    gates[:, 0:SLOTS] = gates_high
+    gates[:, SLOTS:] = (both_gates - gates_high.astype(jnp.float32)).astype(jnp.bfloat16)
 
     load_wq.wait()
 
@@ -299,7 +400,9 @@
     )
     for h in range(KVH):
         v = gathered[:, h * HD : (h + 1) * HD]
-        turned = v * cosine[...] + pltpu.roll(v, HD // 2, 1) * sine[...]
+        cos_q = jnp.concatenate([cosine[0:NEW_DEV]] * 2, axis=0)
+        sin_q = jnp.concatenate([sine[0:NEW_DEV]] * 2, axis=0)
+        turned = v * cos_q + pltpu.roll(v, HD // 2, 1) * sin_q
         queries[h, 0:ROWS] = turned.astype(jnp.bfloat16)
 
     def qx_copy(h):
@@ -315,7 +418,6 @@
         qx_copy(h).start()
     for off in range(1, 8):
         bias_copy(off).wait_recv()
-    load_kv.wait()
 
     lead = (
         lax.broadcasted_iota(jnp.int32, (ROWS, NEW_DEV), 0) % NEW_DEV
@@ -513,20 +615,21 @@
         q_copy(off).wait_send()
 
 
-def layer(kv_own, bias_own, rows_send, gather_q, spread_q, gates, cosine, sine, tokens, wq, wo):
+def layer(*operands):
     bf = jnp.bfloat16
     f32 = jnp.float32
     anywhere = pl.BlockSpec(memory_space=pl.ANY)
     inside = pl.BlockSpec(memory_space=pltpu.VMEM)
+    scalars = pl.BlockSpec(memory_space=pltpu.SMEM)
     dma = pltpu.SemaphoreType.DMA
     return pl.pallas_call(
         kernel,
         out_shape=jax.ShapeDtypeStruct((NEW_DEV, D), bf),
-        in_specs=[anywhere, inside, anywhere] + [inside] * 6 + [anywhere] * 2,
+        in_specs=[scalars] * 3 + [inside] * 7 + [anywhere] * 6,
         out_specs=inside,
         scratch_shapes=[
             pltpu.VMEM((KVH, 2 * NZ, KEYS, 2 * HD), bf),
-            pltpu.VMEM((2 * NZ, 8, 384), f32),
+            pltpu.VMEM((2 * NZ, 8, BIAS_WIDTH), f32),
             pltpu.VMEM((KC, EXPERTS, CAP, KW), bf),
             pltpu.VMEM((D, KVW), bf),
             pltpu.VMEM((KVW, D), bf),
@@ -544,7 +647,19 @@
             pltpu.VMEM((KVH, EXPERTS, CAP, HD), bf),
             pltpu.VMEM((NC, EXPERTS, CAP, NW), bf),
             pltpu.VMEM((NC, EXPERTS, CAP, NW), bf),
-            dma((20,)),
+            pltpu.VMEM((PAIRS, D, PAIR), bf),
+            pltpu.VMEM((PAIRS, D, PAIR), bf),
+            pltpu.VMEM((CACHE_DEV, KVW), bf),
+            pltpu.VMEM((CACHE_DEV, KVW), bf),
+            pltpu.VMEM((NEW_DEV + CB, D), bf),
+            pltpu.VMEM((KC, EXPERTS, CAP, KW), bf),
+            pltpu.VMEM((8, BIAS_WIDTH), f32),
+            pltpu.VMEM((ROWS, SLOTS), bf),
+            pltpu.VMEM((SLOTS, ROWS), bf),
+            pltpu.VMEM((NEW_DEV, 2 * SLOTS), bf),
+            pltpu.VMEM((NEW_DEV + CB, HD), f32),
+            pltpu.VMEM((NEW_DEV + CB, HD), f32),
+            dma((32,)),
             dma((KC, 8)),
             dma((KC, 8)),
             dma((8,)),
@@ -565,10 +680,10 @@
             dma((NC, 8)),
         ],
         compiler_params=pltpu.CompilerParams(
-            collective_id=0, has_side_effects=True, vmem_limit_bytes=60 * 1024 * 1024
+            collective_id=0, has_side_effects=True, vmem_limit_bytes=63 * 1024 * 1024
         ),
         name="layer",
-    )(kv_own, bias_own, rows_send, gather_q, spread_q, gates, cosine, sine, tokens, wq, wo)
+    )(*operands)
 
 
 def shards(
@@ -587,71 +702,34 @@
     block_live,
     cached_len,
 ):
-    bf = jnp.bfloat16
-    f32 = jnp.float32
     blk_index = lax.axis_index("blk")
-    length = cached_len[0]
-    tokens = new_tokens[0]
-    normed = normalize(tokens, norm_gain)
-    held_norm = normalize(hidden_held[0], norm_gain)
-    new_pos = length + blk_index * NEW_DEV + jnp.arange(NEW_DEV, dtype=jnp.int32)
-    held_start = recompute_ids[0, 0] * CB
-    held_pos = blk_index * CACHE_DEV + held_start + jnp.arange(CB, dtype=jnp.int32)
-    both_rows = jnp.concatenate([normed, held_norm], axis=0)
-    cosine, sine = rope_tables(jnp.concatenate([new_pos, held_pos]))
-    key_proj = rotate(
-        jnp.dot(both_rows, w_key, preferred_element_type=f32), cosine, sine
-    ).astype(bf)
-    value_proj = (
-        jnp.dot(both_rows, w_value, preferred_element_type=f32).astype(bf).reshape(-1, KVH, HD)
+    frequency = jnp.exp(
+        (jnp.arange(HD, dtype=jnp.int32) % (HD // 2)).astype(jnp.float32)
+        * (-math.log(theta_base) / (HD // 2))
     )
-    fresh = jnp.concatenate([key_proj, value_proj], axis=-1).transpose(1, 0, 2)
-    cached = jnp.concatenate(
-        [cache_keys[0].reshape(-1, KVH, HD), cache_values[0].reshape(-1, KVH, HD)], axis=-1
-    ).transpose(1, 0, 2)
-    kv_own = jnp.concatenate([fresh[:, :NEW_DEV], cached], axis=1)
-    kv_own = lax.dynamic_update_slice(
-        kv_own, fresh[:, NEW_DEV:], (0, NEW_DEV + held_start, 0)
-    )
-    slot_pos = blk_index * CACHE_DEV + jnp.arange(CACHE_DEV, dtype=jnp.int32)
-    usable = (slot_pos < length) & (jnp.repeat(block_live[0], CB) == 1)
-    bias_own = jnp.where(usable, 0.0, MASKED).astype(f32)
-    bias_own = jnp.broadcast_to(jnp.pad(bias_own, (0, 384 - CACHE_DEV))[None], (8, 384))
-
-    logits = jnp.dot(normed, router_weight, preferred_element_type=f32)
-    picked = att_choice[0]
-    ids = jnp.arange(EXPERTS, dtype=jnp.int32)
-    one_hot = picked.T.reshape(-1)[:, None] == ids[None, :]
-    chosen = jnp.sum(jnp.where(one_hot, jnp.concatenate([logits, logits], 0), 0.0), axis=1)
-    gate_first = jax.nn.sigmoid(chosen[:NEW_DEV] - chosen[NEW_DEV:])
-    order = jnp.arange(ROWS, dtype=jnp.int32)
-    earlier = (order[:, None] > order[None, :]).astype(bf)
-    before = jnp.dot(earlier, one_hot.astype(bf), preferred_element_type=f32)
-    slot = jnp.sum(jnp.where(one_hot, before, 0.0), axis=1).astype(jnp.int32)
-    target = picked.T.reshape(-1) * CAP + slot
-    slots = jnp.arange(SLOTS, dtype=jnp.int32)
-    gather_q = (target[:, None] == slots[None, :]).astype(bf)
-    spread_q = (slots[:, None] == target[None, :]).astype(bf)
-    spread = spread_q[:, :NEW_DEV] + spread_q[:, NEW_DEV:]
-    rows_send = jnp.dot(spread, normed, preferred_element_type=f32).astype(bf)
-    both_gates = jnp.where(
-        target[:NEW_DEV, None] == slots[None, :], gate_first[:, None], 0.0
-    ) + jnp.where(target[NEW_DEV:, None] == slots[None, :], 1.0 - gate_first[:, None], 0.0)
-    gates_high = both_gates.astype(bf)
-    gates_low = (both_gates - gates_high.astype(f32)).astype(bf)
-    gates = jnp.concatenate([gates_high, gates_low], axis=1)
-    q_cos = jnp.concatenate([cosine[:NEW_DEV]] * 2, 0)
-    q_sin = jnp.concatenate([sine[:NEW_DEV]] * 2, 0)
+    new_base = (cached_len[0] + blk_index * NEW_DEV).astype(jnp.float32) * frequency
+    held_base = (blk_index * CACHE_DEV + recompute_ids[0, 0] * CB).astype(jnp.float32) * frequency
+    angles = jnp.stack([new_base, new_base, held_base, held_base])
+    odd = jnp.arange(4)[:, None] % 2 == 1
+    base = jnp.where(odd, jnp.sin(angles), jnp.cos(angles))
+    wave = np.exp((np.arange(HD) % (HD // 2)) * (-math.log(theta_base) / (HD // 2)))
+    turns = np.arange(NEW_DEV)[:, None] * wave[None, :]
+    step = jnp.asarray(np.stack([np.cos(turns), np.sin(turns)]), jnp.float32)
     mixed = layer(
-        kv_own,
-        bias_own,
-        rows_send.reshape(EXPERTS, CAP, D),
-        gather_q,
-        spread_q,
-        gates,
-        q_cos,
-        q_sin,
-        tokens,
+        cached_len,
+        recompute_ids,
+        block_live,
+        new_tokens[0],
+        hidden_held[0],
+        norm_gain[None, :],
+        att_choice[0],
+        router_weight,
+        base,
+        step,
+        w_key,
+        w_value,
+        cache_keys[0],
+        cache_values[0],
         w_query[0],
         w_out[0],
     )

time: 146 us -> 131 us (0.90)
  other arithmetic: 7.14 us -> 0.68 us
  matrix products: 6.42 us -> 0 us
  local copies, waits for them, and re-layouts: 7.96 us -> 5.06 us
  Pallas kernels: 122 us -> 124 us
    dot_general x5 -> x0, matrix products: 6.42 us -> none  [the longest x1 3.03 us: shards(): jnp.dot(both_rows, w_key, preferred_element_type=f32)]
    convert_element_type x7 -> x0, other arithmetic: 2.67 us -> none  [the longest x2 1.35 us: normalize(): return (widened * inverse * norm_gain).astype(jnp.bfloat16)]
    concatenate x6 -> x0, other arithmetic: 2.41 us -> none  [the longest x1 0.75 us: shards(): gates = jnp.concatenate([gates_high, gates_low], axis=1)]
    unnamed x25 -> x3, local copies, waits for them, and re-layouts: 4.96 us -> 5.06 us
where the time goes in v3:
time: 131 us
  Pallas kernels  124 us (95%)
  local copies, waits for them, and re-layouts  5.06 us (4%)
  between operations  1.32 us (1%)
    pallas_call x1, Pallas kernels, layer(): pl.pallas_call(kernel, out_shape=jax.ShapeDtypeStruct((NEW_DEV, D), bf),...  124 us
    unnamed x3, local copies, waits for them, and re-layouts  5.06 us

profile of v3, /device:TPU:0, one launch (start us, length us, event | category | flops | bytes accessed | tf_op | source)
XLA Modules:
  0.0 130.6 jit_solution(10223290023996352642)
XLA Ops:
  1.3 0.7 cosine_select_fusion.base
  2.0 1.4 %copy.16 = s32[1,128,2]{2,1,0:T(8,128)} copy(s32[1,128,2]{1,2,0:T(2,128)} %param.18) | data formatting | bytes 2048 | tf_op args[3]
  3.4 1.8 %copy.17.router = bf16[2048,8]{1,0:T(8,128)(2,1)} copy(bf16[2048,8]{0,1:T(8,128)(2,1)} %param.17) | data formatting | bytes 65536 | tf_op args[2]
  5.2 123.5 %layer.1 = bf16[128,2048]{1,0:T(8,128)(2,1)} custom-call(s32[1]{0:T(128)} %copy.20.length_ref, s32[1,1]{1,0:T(1,128)S(6)} %copy.19.held_ref, s32[1,10]{1,0:T(1,128)} %live_ref.1, bf16[128,2048]{1,0:T(8,128)(2,1)} %bitcast.17, bf16[32,2048]{1,0:T(8,128)(2,1)} %bitcast.19, f32[1,2048]{1,0:T(1,128)} %bitcast.20, s32[128,2]{1,0:T(8,128)} %bitcast.18, ...), custom_call_target="tpu_custom_call" | custom-call | tf_op jit(solution)/shard_map/layer/pallas_call | solution.py:625
  128.7 1.9 %copy.21 = bf16[1,128,2048]{2,1,0:T(8,128)(2,1)} copy(bf16[1,128,2048]{2,1,0:T(8,128)(2,1)} %bitcast.14) | data formatting | bytes 1048576
  (2 shorter events, 0.0 us)

commit v4 on v3

--- a/solution.py
+++ b/solution.py
@@ -30,6 +30,8 @@
 PAIR = 2 * HD
 BLK_DEV = 10
 BIAS_WIDTH = 384
+EARLY = 6
+PASS_AT = (3, 4, 5, 6, 7)
 
 epsilon = 1e-06
 theta_base = 10000.0
@@ -81,6 +83,7 @@
     att_recv,
     exp_send,
     exp_recv,
+    out_acc,
     wk,
     wv,
     old_k,
@@ -191,40 +194,6 @@
     both[0:NEW_DEV] = norm(tokens[...])
     both[NEW_DEV:] = norm(hidden[...])
 
-    lane = lax.broadcasted_iota(jnp.int32, (NEW_DEV, HD), 1)
-    row = lax.broadcasted_iota(jnp.int32, (NEW_DEV, HD), 0)
-    earlier = (row > lane).astype(jnp.bfloat16)
-    hot = [choice[:, k : k + 1] == lane for k in range(2)]
-    count = [
-        jnp.dot(earlier, jnp.where(m, 1.0, 0.0).astype(jnp.bfloat16), preferred_element_type=jnp.float32)
-        for m in hot
-    ]
-    total = jnp.sum(jnp.where(hot[0], 1.0, 0.0), axis=0, keepdims=True)
-    count[1] = count[1] + total
-    slot_lane = lax.broadcasted_iota(jnp.int32, (NEW_DEV, SLOTS), 1)
-    at_slot = []
-    for k in range(2):
-        slot = jnp.sum(jnp.where(hot[k], count[k], 0.0), axis=1, keepdims=True)
-        target = choice[:, k : k + 1] * CAP + slot.astype(jnp.int32)
-        at_slot.append(slot_lane == target)
-    placed = [jnp.where(m, 1.0, 0.0) for m in at_slot]
-    gather_q[0:NEW_DEV] = placed[0].astype(jnp.bfloat16)
-    gather_q[NEW_DEV:] = placed[1].astype(jnp.bfloat16)
-    spread = [m.T for m in placed]
-    spread_q[:, 0:NEW_DEV] = spread[0].astype(jnp.bfloat16)
-    spread_q[:, NEW_DEV:] = spread[1].astype(jnp.bfloat16)
-    dispatch = (spread[0] + spread[1]).astype(jnp.bfloat16)
-    for k in range(KC):
-        rows_send[k] = (
-            jnp.dot(
-                dispatch,
-                both[0:NEW_DEV, k * KW : (k + 1) * KW],
-                preferred_element_type=jnp.float32,
-            )
-            .astype(jnp.bfloat16)
-            .reshape(EXPERTS, CAP, KW)
-        )
-
     def rows_copy(k, off):
         e = peer(off)
         return remote(
@@ -277,15 +246,6 @@
             bias_r.at[off],
             at_blk((z + off // 2) % NZ, xl, (c + off % 2) % 2),
         )
-
-    def send_rows(k, _):
-        for off in range(1, 8):
-            rows_copy(k, off).start()
-        rows_local(k).start()
-        return 0
-
-    pl.semaphore_wait(barrier, 15)
-    lax.fori_loop(0, KC, send_rows, 0)
 
     cb = base[0:1, :]
     sb = base[1:2, :]
@@ -310,7 +270,7 @@
     load_old_v.wait()
     held = lax.broadcasted_iota(jnp.int32, (CACHE_DEV, HD), 0) // CB == held_ref[0, 0]
 
-    for p in range(PAIRS):
+    def own_pair(p):
         load_wk(p).wait()
         load_wv(p).wait()
         keys = jnp.dot(both[...], wk[p], preferred_element_type=jnp.float32)
@@ -328,13 +288,69 @@
                     jnp.concatenate([new[NEW_DEV:]] * BLK_DEV, axis=0),
                     old[:, h * HD : (h + 1) * HD],
                 )
+
+    def send_pair(p):
         for i in range(2):
             for way in range(3):
                 kv_own_copy(2 * p + i, way).start()
+
+    own_pair(0)
+    pl.semaphore_wait(barrier, 15)
+    send_pair(0)
+
+    lane = lax.broadcasted_iota(jnp.int32, (NEW_DEV, HD), 1)
+    row = lax.broadcasted_iota(jnp.int32, (NEW_DEV, HD), 0)
+    earlier = (row > lane).astype(jnp.bfloat16)
+    named = [
+        jnp.broadcast_to(choice[k : k + 1, :].astype(jnp.float32), (HD, NEW_DEV)).T.astype(jnp.int32)
+        for k in range(2)
+    ]
+    hot = [named[k] == lane for k in range(2)]
+    count = [
+        jnp.dot(earlier, jnp.where(m, 1.0, 0.0).astype(jnp.bfloat16), preferred_element_type=jnp.float32)
+        for m in hot
+    ]
+    total = jnp.sum(jnp.where(hot[0], 1.0, 0.0), axis=0, keepdims=True)
+    count[1] = count[1] + total
+    slot_lane = lax.broadcasted_iota(jnp.int32, (NEW_DEV, SLOTS), 1)
+    at_slot = []
+    for k in range(2):
+        slot = jnp.sum(jnp.where(hot[k], count[k], 0.0), axis=1, keepdims=True)
+        target = named[k][:, 0:1] * CAP + slot.astype(jnp.int32)
+        at_slot.append(slot_lane == target)
+    placed = [jnp.where(m, 1.0, 0.0) for m in at_slot]
+    gather_q[0:NEW_DEV] = placed[0].astype(jnp.bfloat16)
+    gather_q[NEW_DEV:] = placed[1].astype(jnp.bfloat16)
+    spread = [m.T for m in placed]
+    spread_q[:, 0:NEW_DEV] = spread[0].astype(jnp.bfloat16)
+    spread_q[:, NEW_DEV:] = spread[1].astype(jnp.bfloat16)
+    dispatch = (spread[0] + spread[1]).astype(jnp.bfloat16)
+    for k in range(KC):
+        rows_send[k] = (
+            jnp.dot(
+                dispatch,
+                both[0:NEW_DEV, k * KW : (k + 1) * KW],
+                preferred_element_type=jnp.float32,
+            )
+            .astype(jnp.bfloat16)
+            .reshape(EXPERTS, CAP, KW)
+        )
+
+    def send_rows(k, _):
+        for off in range(1, 8):
+            rows_copy(k, off).start()
+        rows_local(k).start()
+        return 0
+
+    lax.fori_loop(0, KC, send_rows, 0)
+
+    for p in range(1, PAIRS):
+        own_pair(p)
+        send_pair(p)
     for off in range(1, 8):
         bias_copy(off).start()
 
-    logits = jnp.dot(both[0:NEW_DEV], router[...], preferred_element_type=jnp.float32)
+    logits = product_nt(both[0:NEW_DEV], router[...])
     chosen = [
         jnp.sum(jnp.where(m[:, 0:EXPERTS], logits, 0.0), axis=1, keepdims=True) for m in hot
     ]
@@ -346,42 +362,6 @@
     gates[:, 0:SLOTS] = gates_high
     gates[:, SLOTS:] = (both_gates - gates_high.astype(jnp.float32)).astype(jnp.bfloat16)
 
-    load_wq.wait()
-
-    def project(k, _):
-        for off in range(1, 8):
-            rows_copy(k, off).wait_recv()
-        rows_local(k).wait()
-        part = jnp.dot(
-            rows[k].reshape(SLOTS, KW),
-            wq[pl.ds(pl.multiple_of(k * KW, KW), KW), :],
-            preferred_element_type=jnp.float32,
-        )
-
-        @pl.when(k == 0)
-        def _():
-            qacc[...] = part
-
-        @pl.when(k > 0)
-        def _():
-            qacc[...] += part
-
-        return 0
-
-    lax.fori_loop(0, KC, project, 0)
-    qsend[...] = qacc[...].astype(jnp.bfloat16).reshape(EXPERTS, CAP, KVW)
-
-    def q_copy(off):
-        r = peer(off)
-        return remote(
-            qsend.at[r], qret.at[expert], qs_s.at[off], qs_r.at[off], at_expert(r)
-        )
-
-    for off in range(1, 8):
-        q_copy(off).start()
-    q_local = pltpu.make_async_copy(qsend.at[expert], qret.at[expert], local_sem.at[7])
-    q_local.start()
-
     def pass_on(h, _):
         for way in range(2):
             kv_own_copy(h, way).wait_recv()
@@ -390,20 +370,53 @@
             kv_share(h, way).start()
         return 0
 
-    lax.fori_loop(0, KVH, pass_on, 0)
-
-    for off in range(1, 8):
-        q_copy(off).wait_recv()
-    q_local.wait()
-    gathered = jnp.dot(
-        gather_q[...], qret[...].reshape(SLOTS, KVW), preferred_element_type=jnp.float32
-    )
-    for h in range(KVH):
-        v = gathered[:, h * HD : (h + 1) * HD]
-        cos_q = jnp.concatenate([cosine[0:NEW_DEV]] * 2, axis=0)
-        sin_q = jnp.concatenate([sine[0:NEW_DEV]] * 2, axis=0)
-        turned = v * cos_q + pltpu.roll(v, HD // 2, 1) * sin_q
-        queries[h, 0:ROWS] = turned.astype(jnp.bfloat16)
+    load_wq.wait()
+
+    def project(k, _):
+        for off in range(1, 8):
+            rows_copy(k, off).wait_recv()
+        rows_local(k).wait()
+
+        @pl.when(k > 0)
+        def _():
+            pass_on(k - 1, 0)
+
+        part = jnp.dot(
+            rows[k].reshape(SLOTS, KW),
+            wq[pl.ds(pl.multiple_of(k * KW, KW), KW), :],
+            preferred_element_type=jnp.float32,
+        )
+
+        @pl.when(k == 0)
+        def _():
+            qacc[...] = part
+
+        @pl.when(k > 0)
+        def _():
+            qacc[...] += part
+
+        return 0
+
+    lax.fori_loop(0, KC, project, 0)
+
+    def q_copy(p, off):
+        r = peer(off)
+        return remote(
+            qsend.at[p, r], qret.at[p, expert], qs_s.at[p, off], qs_r.at[p, off], at_expert(r)
+        )
+
+    def q_local(p):
+        return pltpu.make_async_copy(
+            qsend.at[p, expert], qret.at[p, expert], local_sem.at[30 + p]
+        )
+
+    for p in range(PAIRS):
+        qsend[p] = (
+            qacc[:, p * PAIR : (p + 1) * PAIR].astype(jnp.bfloat16).reshape(EXPERTS, CAP, PAIR)
+        )
+        for off in range(1, 8):
+            q_copy(p, off).start()
+        q_local(p).start()
 
     def qx_copy(h):
         return remote(
@@ -414,8 +427,23 @@
             across,
         )
 
-    for h in range(KVH):
-        qx_copy(h).start()
+    cos_q = jnp.concatenate([cosine[0:NEW_DEV]] * 2, axis=0)
+    sin_q = jnp.concatenate([sine[0:NEW_DEV]] * 2, axis=0)
+    for p in range(PAIRS):
+        lax.fori_loop(PASS_AT[p], PASS_AT[p + 1], pass_on, 0)
+        for off in range(1, 8):
+            q_copy(p, off).wait_recv()
+        q_local(p).wait()
+        gathered = jnp.dot(
+            gather_q[...], qret[p].reshape(SLOTS, PAIR), preferred_element_type=jnp.float32
+        )
+        for i in range(2):
+            v = gathered[:, i * HD : (i + 1) * HD]
+            turned = v * cos_q + pltpu.roll(v, HD // 2, 1) * sin_q
+            queries[2 * p + i, 0:ROWS] = turned.astype(jnp.bfloat16)
+        for i in range(2):
+            qx_copy(2 * p + i).start()
+    lax.fori_loop(PASS_AT[PAIRS], KVH, pass_on, 0)
     for off in range(1, 8):
         bias_copy(off).wait_recv()
 
@@ -541,7 +569,19 @@
         att_local(h).wait()
         return 0
 
-    lax.fori_loop(0, KVH, wait_att, 0)
+    lax.fori_loop(0, EARLY, wait_att, 0)
+    arrived = jnp.concatenate([att_recv[h].reshape(SLOTS, HD) for h in range(EARLY)], axis=1)
+
+    def project_early(n, _):
+        out_acc[n] = jnp.dot(
+            arrived,
+            wo[0 : EARLY * HD, pl.ds(pl.multiple_of(n * NW, NW), NW)],
+            preferred_element_type=jnp.float32,
+        )
+        return 0
+
+    lax.fori_loop(0, NC, project_early, 0)
+    lax.fori_loop(EARLY, KVH, wait_att, 0)
 
     def exp_copy(n, off):
         r = peer(off)
@@ -558,12 +598,12 @@
             exp_send.at[n, expert], exp_recv.at[n, expert], local_sem.at[16 + n]
         )
 
-    arrived = jnp.concatenate([att_recv[h].reshape(SLOTS, HD) for h in range(KVH)], axis=1)
+    late = jnp.concatenate([att_recv[h].reshape(SLOTS, HD) for h in range(EARLY, KVH)], axis=1)
 
     def project_out(n, _):
-        part = jnp.dot(
-            arrived,
-            wo[:, pl.ds(pl.multiple_of(n * NW, NW), NW)],
+        part = out_acc[n] + jnp.dot(
+            late,
+            wo[EARLY * HD :, pl.ds(pl.multiple_of(n * NW, NW), NW)],
             preferred_element_type=jnp.float32,
         )
         exp_send[n] = part.astype(jnp.bfloat16).reshape(EXPERTS, CAP, NW)
@@ -612,7 +652,8 @@
     lax.fori_loop(0, KVH, drain_heads, 0)
     for off in range(1, 8):
         bias_copy(off).wait_send()
-        q_copy(off).wait_send()
+        for p in range(PAIRS):
+            q_copy(p, off).wait_send()
 
 
 def layer(*operands):
@@ -634,8 +675,8 @@
             pltpu.VMEM((D, KVW), bf),
             pltpu.VMEM((KVW, D), bf),
             pltpu.VMEM((SLOTS, KVW), f32),
-            pltpu.VMEM((EXPERTS, CAP, KVW), bf),
-            pltpu.VMEM((EXPERTS, CAP, KVW), bf),
+            pltpu.VMEM((PAIRS, EXPERTS, CAP, PAIR), bf),
+            pltpu.VMEM((PAIRS, EXPERTS, CAP, PAIR), bf),
             pltpu.VMEM((KVH, 2 * ROWS, HD), bf),
             pltpu.VMEM((2 * ROWS, 2 * HD), f32),
             pltpu.VMEM((KVH, ROWS, 2 * HD), f32),
@@ -647,6 +688,7 @@
             pltpu.VMEM((KVH, EXPERTS, CAP, HD), bf),
             pltpu.VMEM((NC, EXPERTS, CAP, NW), bf),
             pltpu.VMEM((NC, EXPERTS, CAP, NW), bf),
+            pltpu.VMEM((NC, SLOTS, NW), f32),
             pltpu.VMEM((PAIRS, D, PAIR), bf),
             pltpu.VMEM((PAIRS, D, PAIR), bf),
             pltpu.VMEM((CACHE_DEV, KVW), bf),
@@ -659,11 +701,11 @@
             pltpu.VMEM((NEW_DEV, 2 * SLOTS), bf),
             pltpu.VMEM((NEW_DEV + CB, HD), f32),
             pltpu.VMEM((NEW_DEV + CB, HD), f32),
-            dma((32,)),
+            dma((40,)),
             dma((KC, 8)),
             dma((KC, 8)),
-            dma((8,)),
-            dma((8,)),
+            dma((PAIRS, 8)),
+            dma((PAIRS, 8)),
             dma((KVH, 9)),
             dma((KVH, 9)),
             dma((8,)),
@@ -722,8 +764,8 @@
         new_tokens[0],
         hidden_held[0],
         norm_gain[None, :],
-        att_choice[0],
-        router_weight,
+        att_choice[0].T,
+        router_weight.T,
         base,
         step,
         w_key,

time: 131 us -> 124 us (0.947)
  Pallas kernels: 124 us -> 120 us
  local copies, waits for them, and re-layouts: 5.06 us -> 1.88 us
    pallas_call x1, Pallas kernels: 124 us -> 120 us  [layer(): pl.pallas_call(kernel, out_shape=jax.ShapeDtypeStruct((NEW_DEV, D), bf),...]
    unnamed x3 -> x1, local copies, waits for them, and re-layouts: 5.06 us -> 1.88 us
where the time goes in v4:
time: 124 us
  Pallas kernels  120 us (97%)
  local copies, waits for them, and re-layouts  1.88 us (2%)
  between operations  1.32 us (1%)
    pallas_call x1, Pallas kernels, layer(): pl.pallas_call(kernel, out_shape=jax.ShapeDtypeStruct((NEW_DEV, D), bf),...  120 us

profile of v4, /device:TPU:0, one launch (start us, length us, event | category | flops | bytes accessed | tf_op | source)
XLA Modules:
  0.0 123.9 jit_solution(11140898959576136780)
XLA Ops:
  1.3 0.6 cosine_select_fusion.base
  2.0 120.1 %layer.1 = bf16[128,2048]{1,0:T(8,128)(2,1)} custom-call(s32[1]{0:T(128)} %copy.18.length_ref, s32[1,1]{1,0:T(1,128)S(6)} %copy.17.held_ref, s32[1,10]{1,0:T(1,128)} %live_ref.1, bf16[128,2048]{1,0:T(8,128)(2,1)} %bitcast.20, bf16[32,2048]{1,0:T(8,128)(2,1)} %bitcast.21, f32[1,2048]{1,0:T(1,128)} %bitcast.23, s32[2,128]{1,0:T(2,128)} %bitcast.24, ...), custom_call_target="tpu_custom_call" | custom-call | tf_op jit(solution)/shard_map/layer/pallas_call | solution.py:666
  122.1 1.9 %copy.19 = bf16[1,128,2048]{2,1,0:T(8,128)(2,1)} copy(bf16[1,128,2048]{2,1,0:T(8,128)(2,1)} %bitcast.17) | data formatting | bytes 1048576
  (2 shorter events, 0.0 us)

commit v5 on v4

--- a/solution.py
+++ b/solution.py
@@ -31,6 +31,7 @@
 BLK_DEV = 10
 BIAS_WIDTH = 384
 EARLY = 6
+ORDER = (6, 5, 7, 4, 2, 1, 3)
 PASS_AT = (3, 4, 5, 6, 7)
 
 epsilon = 1e-06
@@ -153,7 +154,7 @@
         )
 
     barrier = pltpu.get_barrier_semaphore()
-    for off in range(1, 8):
+    for off in ORDER:
         pl.semaphore_signal(
             barrier, inc=1, device_id=at_expert(peer(off)), device_id_type=pl.DeviceIdType.MESH
         )
@@ -337,7 +338,7 @@
         )
 
     def send_rows(k, _):
-        for off in range(1, 8):
+        for off in ORDER:
             rows_copy(k, off).start()
         rows_local(k).start()
         return 0
@@ -347,7 +348,7 @@
     for p in range(1, PAIRS):
         own_pair(p)
         send_pair(p)
-    for off in range(1, 8):
+    for off in ORDER:
         bias_copy(off).start()
 
     logits = product_nt(both[0:NEW_DEV], router[...])
@@ -373,7 +374,7 @@
     load_wq.wait()
 
     def project(k, _):
-        for off in range(1, 8):
+        for off in ORDER:
             rows_copy(k, off).wait_recv()
         rows_local(k).wait()
 
@@ -414,7 +415,7 @@
         qsend[p] = (
             qacc[:, p * PAIR : (p + 1) * PAIR].astype(jnp.bfloat16).reshape(EXPERTS, CAP, PAIR)
         )
-        for off in range(1, 8):
+        for off in ORDER:
             q_copy(p, off).start()
         q_local(p).start()
 
@@ -431,7 +432,7 @@
     sin_q = jnp.concatenate([sine[0:NEW_DEV]] * 2, axis=0)
     for p in range(PAIRS):
         lax.fori_loop(PASS_AT[p], PASS_AT[p + 1], pass_on, 0)
-        for off in range(1, 8):
+        for off in ORDER:
             q_copy(p, off).wait_recv()
         q_local(p).wait()
         gathered = jnp.dot(
@@ -444,7 +445,7 @@
         for i in range(2):
             qx_copy(2 * p + i).start()
     lax.fori_loop(PASS_AT[PAIRS], KVH, pass_on, 0)
-    for off in range(1, 8):
+    for off in ORDER:
         bias_copy(off).wait_recv()
 
     lead = (
@@ -515,7 +516,7 @@
         attended = (numerator / denominator).astype(jnp.bfloat16)
         spread = jnp.dot(spread_q[...], attended, preferred_element_type=jnp.float32)
         att_send[h] = spread.astype(jnp.bfloat16).reshape(EXPERTS, CAP, HD)
-        for off in range(1, 8):
+        for off in ORDER:
             att_copy(h, off).start()
         att_local(h).start()
 
@@ -564,7 +565,7 @@
     load_wo.wait()
 
     def wait_att(h, _):
-        for off in range(1, 8):
+        for off in ORDER:
             att_copy(h, off).wait_recv()
         att_local(h).wait()
         return 0
@@ -607,7 +608,7 @@
             preferred_element_type=jnp.float32,
         )
         exp_send[n] = part.astype(jnp.bfloat16).reshape(EXPERTS, CAP, NW)
-        for off in range(1, 8):
+        for off in ORDER:
             exp_copy(n, off).start()
         exp_local(n).start()
         return 0
@@ -615,7 +616,7 @@
     lax.fori_loop(0, NC, project_out, 0)
 
     def combine(n, _):
-        for off in range(1, 8):
+        for off in ORDER:
             exp_copy(n, off).wait_recv()
         exp_local(n).wait()
         back = exp_recv[n].reshape(SLOTS, NW)
@@ -628,7 +629,7 @@
     lax.fori_loop(0, NC, combine, 0)
 
     def drain_rows(k, _):
-        for off in range(1, 8):
+        for off in ORDER:
             rows_copy(k, off).wait_send()
             exp_copy(k, off).wait_send()
         return 0
@@ -645,12 +646,12 @@
         qx_copy(h).wait_send()
         num_copy(h).wait_send()
         den_copy(h).wait_send()
-        for off in range(1, 8):
+        for off in ORDER:
             att_copy(h, off).wait_send()
         return 0
 
     lax.fori_loop(0, KVH, drain_heads, 0)
-    for off in range(1, 8):
+    for off in ORDER:
         bias_copy(off).wait_send()
         for p in range(PAIRS):
             q_copy(p, off).wait_send()

time: 124 us -> 123 us (level)
  no operation moved by 1% of the time
where the time goes in v5:
time: 123 us
  Pallas kernels  119 us (97%)
  local copies, waits for them, and re-layouts  1.88 us (2%)
  between operations  1.32 us (1%)
    pallas_call x1, Pallas kernels, layer(): pl.pallas_call(kernel, out_shape=jax.ShapeDtypeStruct((NEW_DEV, D), bf),...  119 us

profile of v5, /device:TPU:0, one launch (start us, length us, event | category | flops | bytes accessed | tf_op | source)
XLA Modules:
  0.0 122.9 jit_solution(17010460450097013171)
XLA Ops:
  1.3 0.6 cosine_select_fusion.base
  2.0 119.0 %layer.1 = bf16[128,2048]{1,0:T(8,128)(2,1)} custom-call(s32[1]{0:T(128)} %copy.18.length_ref, s32[1,1]{1,0:T(1,128)S(6)} %copy.17.held_ref, s32[1,10]{1,0:T(1,128)} %live_ref.1, bf16[128,2048]{1,0:T(8,128)(2,1)} %bitcast.20, bf16[32,2048]{1,0:T(8,128)(2,1)} %bitcast.21, f32[1,2048]{1,0:T(1,128)} %bitcast.23, s32[2,128]{1,0:T(2,128)} %bitcast.24, ...), custom_call_target="tpu_custom_call" | custom-call | tf_op jit(solution)/shard_map/layer/pallas_call | solution.py:667
  121.0 1.9 %copy.19 = bf16[1,128,2048]{2,1,0:T(8,128)(2,1)} copy(bf16[1,128,2048]{2,1,0:T(8,128)(2,1)} %bitcast.17) | data formatting | bytes 1048576
  (2 shorter events, 0.0 us)

commit v6 on v5

--- a/solution.py
+++ b/solution.py
@@ -32,7 +32,8 @@
 BIAS_WIDTH = 384
 EARLY = 6
 ORDER = (6, 5, 7, 4, 2, 1, 3)
-PASS_AT = (3, 4, 5, 6, 7)
+PASS_AT = {0: 3, 3: 4}
+AHEAD = 3
 
 epsilon = 1e-06
 theta_base = 10000.0
@@ -55,9 +56,9 @@
     hidden,
     gain,
     choice,
-    router,
+    router_far,
     base,
-    step,
+    step_far,
     w_key,
     w_value,
     cache_keys,
@@ -85,6 +86,8 @@
     exp_send,
     exp_recv,
     out_acc,
+    router,
+    step,
     wk,
     wv,
     old_k,
@@ -179,6 +182,9 @@
 
     load_old_k = pltpu.make_async_copy(cache_keys, old_k, local_sem.at[28])
     load_old_v = pltpu.make_async_copy(cache_values, old_v, local_sem.at[29])
+    load_step = pltpu.make_async_copy(step_far, step, local_sem.at[34])
+    load_router = pltpu.make_async_copy(router_far, router, local_sem.at[35])
+    load_step.start()
     load_old_k.start()
     load_old_v.start()
     for p in range(PAIRS):
@@ -186,6 +192,7 @@
         load_wv(p).start()
     load_wq.start()
     load_wo.start()
+    load_router.start()
 
     def norm(hidden_rows):
         widened = hidden_rows.astype(jnp.float32)
@@ -252,6 +259,7 @@
     sb = base[1:2, :]
     ch = base[2:3, :]
     sh = base[3:4, :]
+    load_step.wait()
     ct = step[0]
     st = step[1]
     sign = jnp.where(lax.broadcasted_iota(jnp.int32, (1, HD), 1) < HD // 2, -1.0, 1.0)
@@ -291,9 +299,9 @@
                 )
 
     def send_pair(p):
-        for i in range(2):
+        for h in range(2 * p, min(2 * p + 2, AHEAD)):
             for way in range(3):
-                kv_own_copy(2 * p + i, way).start()
+                kv_own_copy(h, way).start()
 
     own_pair(0)
     pl.semaphore_wait(barrier, 15)
@@ -351,6 +359,7 @@
     for off in ORDER:
         bias_copy(off).start()
 
+    load_router.wait()
     logits = product_nt(both[0:NEW_DEV], router[...])
     chosen = [
         jnp.sum(jnp.where(m[:, 0:EXPERTS], logits, 0.0), axis=1, keepdims=True) for m in hot
@@ -363,13 +372,15 @@
     gates[:, 0:SLOTS] = gates_high
     gates[:, SLOTS:] = (both_gates - gates_high.astype(jnp.float32)).astype(jnp.bfloat16)
 
-    def pass_on(h, _):
+    def pass_on(h, more):
         for way in range(2):
             kv_own_copy(h, way).wait_recv()
             kv_forward(h, way).start()
         for way in range(2):
             kv_share(h, way).start()
-        return 0
+        if more:
+            for way in range(3):
+                kv_own_copy(h + AHEAD, way).start()
 
     load_wq.wait()
 
@@ -380,7 +391,7 @@
 
         @pl.when(k > 0)
         def _():
-            pass_on(k - 1, 0)
+            pass_on(k - 1, True)
 
         part = jnp.dot(
             rows[k].reshape(SLOTS, KW),
@@ -431,7 +442,8 @@
     cos_q = jnp.concatenate([cosine[0:NEW_DEV]] * 2, axis=0)
     sin_q = jnp.concatenate([sine[0:NEW_DEV]] * 2, axis=0)
     for p in range(PAIRS):
-        lax.fori_loop(PASS_AT[p], PASS_AT[p + 1], pass_on, 0)
+        if p in PASS_AT:
+            pass_on(PASS_AT[p], True)
         for off in ORDER:
             q_copy(p, off).wait_recv()
         q_local(p).wait()
@@ -444,7 +456,6 @@
             queries[2 * p + i, 0:ROWS] = turned.astype(jnp.bfloat16)
         for i in range(2):
             qx_copy(2 * p + i).start()
-    lax.fori_loop(PASS_AT[PAIRS], KVH, pass_on, 0)
     for off in ORDER:
         bias_copy(off).wait_recv()
 
@@ -521,6 +532,10 @@
         att_local(h).start()
 
     def one_head(h, _):
+        @pl.when((h % 2 == 0) & (h < 6))
+        def _():
+            pass_on(5 + h // 2, False)
+
         for way in range(2):
             kv_forward(h, way).wait_recv()
             kv_share(h, 2 + way).start()
@@ -667,7 +682,7 @@
     return pl.pallas_call(
         kernel,
         out_shape=jax.ShapeDtypeStruct((NEW_DEV, D), bf),
-        in_specs=[scalars] * 3 + [inside] * 7 + [anywhere] * 6,
+        in_specs=[scalars] * 3 + [inside] * 4 + [anywhere, inside] + [anywhere] * 7,
         out_specs=inside,
         scratch_shapes=[
             pltpu.VMEM((KVH, 2 * NZ, KEYS, 2 * HD), bf),
@@ -690,6 +705,8 @@
             pltpu.VMEM((NC, EXPERTS, CAP, NW), bf),
             pltpu.VMEM((NC, EXPERTS, CAP, NW), bf),
             pltpu.VMEM((NC, SLOTS, NW), f32),
+            pltpu.VMEM((EXPERTS, D), bf),
+            pltpu.VMEM((2, NEW_DEV, HD), f32),
             pltpu.VMEM((PAIRS, D, PAIR), bf),
             pltpu.VMEM((PAIRS, D, PAIR), bf),
             pltpu.VMEM((CACHE_DEV, KVW), bf),

time: 123 us -> 123 us (level)
  no operation moved by 1% of the time
where the time goes in v6:
time: 123 us
  Pallas kernels  119 us (97%)
  local copies, waits for them, and re-layouts  1.88 us (2%)
  between operations  1.32 us (1%)
    pallas_call x1, Pallas kernels, layer(): pl.pallas_call(kernel, out_shape=jax.ShapeDtypeStruct((NEW_DEV, D), bf),...  119 us

profile of v6, /device:TPU:0, one launch (start us, length us, event | category | flops | bytes accessed | tf_op | source)
XLA Modules:
  0.0 122.5 jit_solution(3754374413624561542)
XLA Ops:
  1.3 0.6 cosine_select_fusion.base
  2.0 118.7 %layer.1 = bf16[128,2048]{1,0:T(8,128)(2,1)} custom-call(s32[1]{0:T(128)} %copy.18.length_ref, s32[1,1]{1,0:T(1,128)S(6)} %copy.17.held_ref, s32[1,10]{1,0:T(1,128)} %live_ref.1, bf16[128,2048]{1,0:T(8,128)(2,1)} %bitcast.20, bf16[32,2048]{1,0:T(8,128)(2,1)} %bitcast.21, f32[1,2048]{1,0:T(1,128)} %bitcast.23, s32[2,128]{1,0:T(2,128)} %bitcast.24, ...), custom_call_target="tpu_custom_call" | custom-call | tf_op jit(solution)/shard_map/layer/pallas_call | solution.py:682
  120.6 1.9 %copy.19 = bf16[1,128,2048]{2,1,0:T(8,128)(2,1)} copy(bf16[1,128,2048]{2,1,0:T(8,128)(2,1)} %bitcast.17) | data formatting | bytes 1048576
  (2 shorter events, 0.0 us)
